TPU v7x, 128 devices: a whole 4x4x4 slice. The times are simulated.
128 devices in a mesh: asc: 16 (over y, x), desc: 8 (over z, core).
Axes of the slice: x: 4, y: 4, z: 4, core: 2. Of those that a mesh axis runs over, the one named last changes fastest.
Arguments:
- coef_asc: float32 [4096, 128], P(('asc', 'desc')), may hold values from -0.3 to 0.3
- coef_desc: float32 [4096, 128], P(('asc', 'desc')), may hold values from -0.3 to 0.3
- cross_asc: int32 [8192, 128], P(('asc', 'desc')), may hold values from 0 to 4095, as said below
- cross_desc: int32 [8192, 128], P(('asc', 'desc')), may hold values from 0 to 4095, as said below
- time_asc: float32 [8192, 128], P(('asc', 'desc')), may hold values from 0 to 1
- time_desc: float32 [8192, 128], P(('asc', 'desc')), may hold values from 0 to 1
- height: float32 [8192, 128], P(('asc', 'desc')), may hold values from -18 to 18
- block_fill: int32 [8192], P(('asc', 'desc')), may hold values from 0 to 128, as said below
Outputs:
- adjusted_asc: float32 [4096, 128], P(('asc', 'desc'))
- adjusted_desc: float32 [4096, 128], P(('asc', 'desc'))
Inputs may be any that keep to these rules, and one draw needn't show every extreme that they name: `cross_asc`: every crossover slot stored on a device of asc index p names an ascending arc a with a // 256 == p; slot s of every block names an arc a with (a // 32) % 8 == s % 8. `cross_desc`: every crossover slot stored on a device of desc index q names a descending arc d with (d // 32) % 8 == q; slot s of every block names an arc d with d // 256 == s % 16. `block_fill`: the slots in use stand first in each block; on each device the blocks with a nonzero count stand first and the first block is full; on some device all 64 blocks are in use.
All inputs are finite; a program needn't handle non-finite values.
Results may differ from a plain program's by a relative error of at most 0.0003.
Values sent between devices are 32-bit elements; how exact they have to be, the bound alone decides.
A program may use at most 64 MiB of HBM per device.

v0:
```python
import functools

import jax
import jax.numpy as jnp
from jax import lax
from jax.sharding import Mesh
from jax.sharding import PartitionSpec as P

GN_STEPS = 2
CG_STEPS = 3
ASC_DESC = ("asc_0", "asc_1", "desc_0", "desc_1")
ASC = ("asc_0", "asc_1")
DESC = ("desc_0", "desc_1")


damping = 2.0
cauchy_square = 2.25


def by_axis(shard, axes):
    return functools.reduce(lax.psum, axes, shard)


def side_by_side(arrays, axis, split_dim, concat_dim, along):
    ends, at = ([], 0)
    for a in arrays[:-1]:
        at += a.shape[along]
        ends.append(at)
    both = jnp.concatenate(arrays, axis=along)
    return tuple(
        jnp.split(
            lax.all_to_all(both, axis, split_axis=split_dim, concat_axis=concat_dim, tiled=True),
            ends,
            axis=along,
        )
    )


def harmonics(times, term_count):
    half_terms = term_count // 2
    frequency = (lax.iota(jnp.int32, half_terms) + 1).astype(jnp.float32)
    phases = jnp.pi * times[:, None] * frequency[None, :]
    return jnp.concatenate([jnp.cos(phases), jnp.sin(phases)], axis=1)


def one_hot(ids, count):
    return (ids[:, None] == lax.iota(jnp.int32, count)[None, :]).astype(jnp.float32)


def pick_rows(selector, field):
    return jnp.dot(
        selector, field, precision=lax.Precision.HIGHEST, preferred_element_type=jnp.float32
    )


def collect_rows(selector, terms):
    return lax.dot_general(
        selector,
        terms,
        (((0,), (0,)), ((), ())),
        precision=lax.Precision.HIGHEST,
        preferred_element_type=jnp.float32,
    )


def residual_react(modelled, observed, live_mask, previous):
    misfit = live_mask * (observed - modelled)
    weight = live_mask / (1.0 + misfit * misfit / cauchy_square)
    return (weight * misfit, weight, jnp.zeros((), jnp.float32))


def image_react(modelled, observed, live_mask, previous):
    weighted = previous * modelled
    curve_part = jnp.sum(weighted * modelled)
    return (weighted, previous, curve_part)


def norm_total(value):
    return by_axis(value, ASC_DESC)


def curve_total(value):
    return by_axis(value, ASC_DESC)


def body(coef_asc, coef_desc, cross_asc, cross_desc, time_asc, time_desc, height, block_fill):
    owned_asc, term_count = coef_asc.shape
    owned_desc = coef_desc.shape[0]
    blocks, block_width = cross_asc.shape
    count_asc = lax.axis_size(ASC)
    count_desc = lax.axis_size(DESC)
    position = lax.broadcasted_iota(jnp.int32, (blocks, block_width), 1)
    live_plain = (position < block_fill[:, None]).astype(jnp.float32)
    cols_asc = block_width // count_desc
    cols_desc = block_width // count_asc
    ids_send_asc = (cross_asc % owned_asc).astype(jnp.float32).reshape(blocks, cols_asc, count_desc)
    got_ids_asc, got_times_asc = side_by_side(
        (ids_send_asc, time_asc.reshape(blocks, cols_asc, count_desc)), DESC, 2, 2, 0
    )
    ids_send_desc = (
        (cross_desc % owned_desc).astype(jnp.float32).reshape(blocks, cols_desc, count_asc)
    )
    got_ids_desc, got_times_desc = side_by_side(
        (ids_send_desc, time_desc.reshape(blocks, cols_desc, count_asc)), ASC, 2, 2, 0
    )
    select_asc = one_hot(got_ids_asc.reshape(-1).astype(jnp.int32), owned_asc)
    select_desc = one_hot(got_ids_desc.reshape(-1).astype(jnp.int32), owned_desc)
    holder_basis_asc = harmonics(got_times_asc.reshape(-1), term_count)
    holder_basis_desc = harmonics(got_times_desc.reshape(-1), term_count)
    state_asc, state_desc = (coef_asc, coef_desc)
    keep_asc = jnp.float32(1.0)
    keep_desc = jnp.float32(1.0)
    empty_weights = jnp.zeros((blocks, block_width), jnp.float32)

    def crossing(field_asc, field_desc, react, weights):
        value_asc = jnp.sum(holder_basis_asc * pick_rows(select_asc, field_asc), axis=1)
        value_desc = jnp.sum(holder_basis_desc * pick_rows(select_desc, field_desc), axis=1)
        back_asc = lax.all_to_all(
            value_asc.reshape(blocks, cols_asc, count_desc),
            DESC,
            split_axis=2,
            concat_axis=2,
            tiled=True,
        ).reshape(blocks, block_width)
        back_desc = lax.all_to_all(
            value_desc.reshape(blocks, cols_desc, count_asc),
            ASC,
            split_axis=2,
            concat_axis=2,
            tiled=True,
        ).reshape(blocks, block_width)
        weighted, weight, curve_part = react(back_asc - back_desc, height, live_plain, weights)
        out_asc = lax.all_to_all(
            weighted.reshape(blocks, cols_asc, count_desc),
            DESC,
            split_axis=2,
            concat_axis=2,
            tiled=True,
        ).reshape(-1)
        out_desc = lax.all_to_all(
            weighted.reshape(blocks, cols_desc, count_asc),
            ASC,
            split_axis=2,
            concat_axis=2,
            tiled=True,
        ).reshape(-1)
        grad_asc = collect_rows(select_asc, out_asc[:, None] * holder_basis_asc)
        grad_desc = -collect_rows(select_desc, out_desc[:, None] * holder_basis_desc)
        return (grad_asc, grad_desc, curve_part, weight)

    def inner_sum(first, second):
        return keep_asc * jnp.sum(first[0] * second[0]) + keep_desc * jnp.sum(first[1] * second[1])

    for outer_step in range(GN_STEPS):
        grad_asc, grad_desc, unused, weights = crossing(
            state_asc, state_desc, residual_react, empty_weights
        )
        remainder = (grad_asc - damping * state_asc, grad_desc - damping * state_desc)
        direction = remainder
        step_sum = (jnp.zeros_like(state_asc), jnp.zeros_like(state_desc))
        norm_now = norm_total(inner_sum(remainder, remainder))
        for inner_step in range(CG_STEPS):
            image_asc, image_desc, curve_part, kept = crossing(
                direction[0], direction[1], image_react, weights
            )
            image_pair = (image_asc + damping * direction[0], image_desc + damping * direction[1])
            curvature = curve_total(curve_part + damping * inner_sum(direction, direction))
            step_length = norm_now / curvature
            step_sum = (
                step_sum[0] + step_length * direction[0],
                step_sum[1] + step_length * direction[1],
            )
            if inner_step + 1 < CG_STEPS:
                remainder = (
                    remainder[0] - step_length * image_pair[0],
                    remainder[1] - step_length * image_pair[1],
                )
                norm_next = norm_total(inner_sum(remainder, remainder))
                ratio = norm_next / norm_now
                direction = (
                    remainder[0] + ratio * direction[0],
                    remainder[1] + ratio * direction[1],
                )
                norm_now = norm_next
        state_asc = state_asc + step_sum[0]
        state_desc = state_desc + step_sum[1]
    result_asc, result_desc = (state_asc, state_desc)
    return (result_asc, result_desc)


def solution(mesh):
    torus = Mesh(mesh.devices.reshape(4, 4, 4, 2), ("asc_0", "asc_1", "desc_0", "desc_1"))
    placed = (
        P(ASC_DESC, None),
        P(ASC_DESC, None),
        P(ASC_DESC, None),
        P(ASC_DESC, None),
        P(ASC_DESC, None),
        P(ASC_DESC, None),
        P(ASC_DESC, None),
        P(ASC_DESC),
    )
    return jax.shard_map(
        body,
        mesh=torus,
        in_specs=placed,
        out_specs=(P(ASC_DESC, None), P(ASC_DESC, None)),
        check_vma=False,
    )
```

profile of v0, /device:TPU:0, one launch (start us, length us, event | category | flops | bytes accessed | tf_op | source)
XLA Modules:
  0.0 765.3 jit_solution(3258072133698222782)
XLA Ops:
  3.1 5.4 all-to-all-start
  14.2 7.0 all-to-all-start.2
  22.4 6.5 all-to-all-done.2
  29.3 15.6 %multiply_cosine_fusion.1 = (f32[8192,64]{0,1:T(8,128)S(1)}, f32[8192,64]{0,1:T(8,128)S(1)}, f32[8192,64]{0,1:T(8,128)S(1)}, f32[8192,64]{0,1:T(8,128)}) fusion(f32[64]{0:T(128)S(1)} %add_convert_fusion, f32[8192]{0:T(1024)S(1)} %mul.521, f32[8192]{0:T(1024)S(1)} %mul.527), kind=kLoop, calls=%fused_computation.45 | loop fusion | flops 1048576 | bytes 8454400 | tf_op jit(solution)/shard_map/cos | solution.py:43
  63.9 6.1 all-to-all-done.3
  86.3 5.5 multiply_reduce_fusion.23
  107.6 7.3 all-to-all-start.7
  115.6 6.8 all-to-all-done.7
  131.2 9.4 %all-reduce.5 = (f32[]{:T(128)}, f32[]{:T(128)}) all-reduce(f32[]{:T(128)S(6)} %add.260, f32[]{:T(128)S(6)} %add.261), channel_id=1, replica_groups=mesh['asc_0'=4,'asc_1'=4,'desc_0'=4,'desc_1'=2] {'asc_0'}, use_global_device_ids=true, to_apply=%region_4.5 | all-reduce | flops 2 | bytes 16 | tf_op jit(solution)/shard_map/psum | solution.py:21
  140.7 9.6 %all-reduce.3 = (f32[]{:T(128)}, f32[]{:T(128)}) all-reduce(f32[]{:T(128)} %get-tuple-element.12, f32[]{:T(128)} %get-tuple-element.13), channel_id=1, replica_groups=mesh['asc_0'=4,'asc_1'=4,'desc_0'=4,'desc_1'=2] {'asc_1'}, use_global_device_ids=true, to_apply=%region_5.6 | all-reduce | flops 2 | bytes 16 | tf_op jit(solution)/shard_map/psum | solution.py:21
  150.3 11.6 %all-reduce.1 = (f32[]{:T(128)}, f32[]{:T(128)}) all-reduce(f32[]{:T(128)} %get-tuple-element.8, f32[]{:T(128)} %get-tuple-element.9), channel_id=1, replica_groups=mesh['asc_0'=4,'asc_1'=4,'desc_0'=4,'desc_1'=2] {'desc_0'}, use_global_device_ids=true, to_apply=%region_6.7 | all-reduce | flops 2 | bytes 16 | tf_op jit(solution)/shard_map/psum | solution.py:21
  172.0 5.2 multiply_reduce_fusion.21
  185.2 10.6 %psum.344 = f32[]{:T(128)} all-reduce(f32[]{:T(128)S(6)} %add.264), channel_id=1, replica_groups=mesh['asc_0'=4,'asc_1'=4,'desc_0'=4,'desc_1'=2] {'asc_0'}, use_global_device_ids=true, to_apply=%region_17.18 | all-reduce | flops 1 | bytes 8 | tf_op jit(solution)/shard_map/psum | solution.py:21
  195.8 11.1 %psum.345 = f32[]{:T(128)} all-reduce(f32[]{:T(128)} %psum.344), channel_id=1, replica_groups=mesh['asc_0'=4,'asc_1'=4,'desc_0'=4,'desc_1'=2] {'asc_1'}, use_global_device_ids=true, to_apply=%region_18.19 | all-reduce | flops 1 | bytes 8 | tf_op jit(solution)/shard_map/psum | solution.py:21
  206.9 8.4 %psum.346 = f32[]{:T(128)} all-reduce(f32[]{:T(128)} %psum.345), channel_id=1, replica_groups=mesh['asc_0'=4,'asc_1'=4,'desc_0'=4,'desc_1'=2] {'desc_0'}, use_global_device_ids=true, to_apply=%region_19.20 | all-reduce | flops 1 | bytes 8 | tf_op jit(solution)/shard_map/psum | solution.py:21
  239.5 6.7 all-to-all-done.11
  254.3 9.4 %psum.348 = f32[]{:T(128)} all-reduce(f32[]{:T(128)S(6)} %add.268), channel_id=1, replica_groups=mesh['asc_0'=4,'asc_1'=4,'desc_0'=4,'desc_1'=2] {'asc_0'}, use_global_device_ids=true, to_apply=%region_26.27 | all-reduce | flops 1 | bytes 8 | tf_op jit(solution)/shard_map/psum | solution.py:21
  263.6 9.5 %psum.349 = f32[]{:T(128)} all-reduce(f32[]{:T(128)} %psum.348), channel_id=1, replica_groups=mesh['asc_0'=4,'asc_1'=4,'desc_0'=4,'desc_1'=2] {'asc_1'}, use_global_device_ids=true, to_apply=%region_27.28 | all-reduce | flops 1 | bytes 8 | tf_op jit(solution)/shard_map/psum | solution.py:21
  273.2 11.6 %psum.350 = f32[]{:T(128)} all-reduce(f32[]{:T(128)} %psum.349), channel_id=1, replica_groups=mesh['asc_0'=4,'asc_1'=4,'desc_0'=4,'desc_1'=2] {'desc_0'}, use_global_device_ids=true, to_apply=%region_28.29 | all-reduce | flops 1 | bytes 8 | tf_op jit(solution)/shard_map/psum | solution.py:21
  295.2 5.2 multiply_reduce_fusion.17
  308.4 10.5 %psum.352 = f32[]{:T(128)} all-reduce(f32[]{:T(128)S(6)} %add.272), channel_id=1, replica_groups=mesh['asc_0'=4,'asc_1'=4,'desc_0'=4,'desc_1'=2] {'asc_0'}, use_global_device_ids=true, to_apply=%region_32.33 | all-reduce | flops 1 | bytes 8 | tf_op jit(solution)/shard_map/psum | solution.py:21
  318.9 11.0 %psum.353 = f32[]{:T(128)} all-reduce(f32[]{:T(128)} %psum.352), channel_id=1, replica_groups=mesh['asc_0'=4,'asc_1'=4,'desc_0'=4,'desc_1'=2] {'asc_1'}, use_global_device_ids=true, to_apply=%region_33.34 | all-reduce | flops 1 | bytes 8 | tf_op jit(solution)/shard_map/psum | solution.py:21
  329.9 8.3 %psum.354 = f32[]{:T(128)} all-reduce(f32[]{:T(128)} %psum.353), channel_id=1, replica_groups=mesh['asc_0'=4,'asc_1'=4,'desc_0'=4,'desc_1'=2] {'desc_0'}, use_global_device_ids=true, to_apply=%region_34.35 | all-reduce | flops 1 | bytes 8 | tf_op jit(solution)/shard_map/psum | solution.py:21
  370.0 9.4 %psum.356 = f32[]{:T(128)} all-reduce(f32[]{:T(128)S(6)} %add.276), channel_id=1, replica_groups=mesh['asc_0'=4,'asc_1'=4,'desc_0'=4,'desc_1'=2] {'asc_0'}, use_global_device_ids=true, to_apply=%region_41.42 | all-reduce | flops 1 | bytes 8 | tf_op jit(solution)/shard_map/psum | solution.py:21
  379.4 9.5 %psum.357 = f32[]{:T(128)} all-reduce(f32[]{:T(128)} %psum.356), channel_id=1, replica_groups=mesh['asc_0'=4,'asc_1'=4,'desc_0'=4,'desc_1'=2] {'asc_1'}, use_global_device_ids=true, to_apply=%region_42.43 | all-reduce | flops 1 | bytes 8 | tf_op jit(solution)/shard_map/psum | solution.py:21
  388.9 11.3 %psum.358 = f32[]{:T(128)} all-reduce(f32[]{:T(128)} %psum.357), channel_id=1, replica_groups=mesh['asc_0'=4,'asc_1'=4,'desc_0'=4,'desc_1'=2] {'desc_0'}, use_global_device_ids=true, to_apply=%region_43.44 | all-reduce | flops 1 | bytes 8 | tf_op jit(solution)/shard_map/psum | solution.py:21
  423.2 6.7 all-to-all-done.17
  445.7 5.5 multiply_reduce_fusion.13
  467.1 7.2 all-to-all-start.21
  475.1 6.8 all-to-all-done.21
  490.7 9.4 %all-reduce.4 = (f32[]{:T(128)}, f32[]{:T(128)}) all-reduce(f32[]{:T(128)S(6)} %add.283, f32[]{:T(128)S(6)} %add.284), channel_id=1, replica_groups=mesh['asc_0'=4,'asc_1'=4,'desc_0'=4,'desc_1'=2] {'asc_0'}, use_global_device_ids=true, to_apply=%region_49.50 | all-reduce | flops 2 | bytes 16 | tf_op jit(solution)/shard_map/psum | solution.py:21
  500.2 9.6 %all-reduce.2 = (f32[]{:T(128)}, f32[]{:T(128)}) all-reduce(f32[]{:T(128)} %get-tuple-element.10, f32[]{:T(128)} %get-tuple-element.11), channel_id=1, replica_groups=mesh['asc_0'=4,'asc_1'=4,'desc_0'=4,'desc_1'=2] {'asc_1'}, use_global_device_ids=true, to_apply=%region_50.51 | all-reduce | flops 2 | bytes 16 | tf_op jit(solution)/shard_map/psum | solution.py:21
  509.8 11.6 %all-reduce = (f32[]{:T(128)}, f32[]{:T(128)}) all-reduce(f32[]{:T(128)} %get-tuple-element.6, f32[]{:T(128)} %get-tuple-element.7), channel_id=1, replica_groups=mesh['asc_0'=4,'asc_1'=4,'desc_0'=4,'desc_1'=2] {'desc_0'}, use_global_device_ids=true, to_apply=%region_51.52 | all-reduce | flops 2 | bytes 16 | tf_op jit(solution)/shard_map/psum | solution.py:21
  531.3 5.2 multiply_reduce_fusion.11
  544.5 10.4 %psum.368 = f32[]{:T(128)} all-reduce(f32[]{:T(128)S(6)} %add.287), channel_id=1, replica_groups=mesh['asc_0'=4,'asc_1'=4,'desc_0'=4,'desc_1'=2] {'asc_0'}, use_global_device_ids=true, to_apply=%region_62.63 | all-reduce | flops 1 | bytes 8 | tf_op jit(solution)/shard_map/psum | solution.py:21
  555.0 11.1 %psum.369 = f32[]{:T(128)} all-reduce(f32[]{:T(128)} %psum.368), channel_id=1, replica_groups=mesh['asc_0'=4,'asc_1'=4,'desc_0'=4,'desc_1'=2] {'asc_1'}, use_global_device_ids=true, to_apply=%region_63.64 | all-reduce | flops 1 | bytes 8 | tf_op jit(solution)/shard_map/psum | solution.py:21
  566.1 8.4 %psum.370 = f32[]{:T(128)} all-reduce(f32[]{:T(128)} %psum.369), channel_id=1, replica_groups=mesh['asc_0'=4,'asc_1'=4,'desc_0'=4,'desc_1'=2] {'desc_0'}, use_global_device_ids=true, to_apply=%region_64.65 | all-reduce | flops 1 | bytes 8 | tf_op jit(solution)/shard_map/psum | solution.py:21
  599.1 6.7 all-to-all-done.25
  613.8 9.4 %psum.372 = f32[]{:T(128)} all-reduce(f32[]{:T(128)S(6)} %add.291), channel_id=1, replica_groups=mesh['asc_0'=4,'asc_1'=4,'desc_0'=4,'desc_1'=2] {'asc_0'}, use_global_device_ids=true, to_apply=%region_71.72 | all-reduce | flops 1 | bytes 8 | tf_op jit(solution)/shard_map/psum | solution.py:21
  623.2 9.5 %psum.373 = f32[]{:T(128)} all-reduce(f32[]{:T(128)} %psum.372), channel_id=1, replica_groups=mesh['asc_0'=4,'asc_1'=4,'desc_0'=4,'desc_1'=2] {'asc_1'}, use_global_device_ids=true, to_apply=%region_72.73 | all-reduce | flops 1 | bytes 8 | tf_op jit(solution)/shard_map/psum | solution.py:21
  632.7 11.6 %psum.374 = f32[]{:T(128)} all-reduce(f32[]{:T(128)} %psum.373), channel_id=1, replica_groups=mesh['asc_0'=4,'asc_1'=4,'desc_0'=4,'desc_1'=2] {'desc_0'}, use_global_device_ids=true, to_apply=%region_73.74 | all-reduce | flops 1 | bytes 8 | tf_op jit(solution)/shard_map/psum | solution.py:21
  654.4 5.2 multiply_reduce_fusion.7
  667.6 10.4 %psum.376 = f32[]{:T(128)} all-reduce(f32[]{:T(128)S(6)} %add.295), channel_id=1, replica_groups=mesh['asc_0'=4,'asc_1'=4,'desc_0'=4,'desc_1'=2] {'asc_0'}, use_global_device_ids=true, to_apply=%region_77.78 | all-reduce | flops 1 | bytes 8 | tf_op jit(solution)/shard_map/psum | solution.py:21
  678.0 11.0 %psum.377 = f32[]{:T(128)} all-reduce(f32[]{:T(128)} %psum.376), channel_id=1, replica_groups=mesh['asc_0'=4,'asc_1'=4,'desc_0'=4,'desc_1'=2] {'asc_1'}, use_global_device_ids=true, to_apply=%region_78.79 | all-reduce | flops 1 | bytes 8 | tf_op jit(solution)/shard_map/psum | solution.py:21
  689.0 8.3 %psum.378 = f32[]{:T(128)} all-reduce(f32[]{:T(128)} %psum.377), channel_id=1, replica_groups=mesh['asc_0'=4,'asc_1'=4,'desc_0'=4,'desc_1'=2] {'desc_0'}, use_global_device_ids=true, to_apply=%region_79.80 | all-reduce | flops 1 | bytes 8 | tf_op jit(solution)/shard_map/psum | solution.py:21
  729.3 9.4 %psum.380 = f32[]{:T(128)} all-reduce(f32[]{:T(128)S(6)} %add.299), channel_id=1, replica_groups=mesh['asc_0'=4,'asc_1'=4,'desc_0'=4,'desc_1'=2] {'asc_0'}, use_global_device_ids=true, to_apply=%region_86.87 | all-reduce | flops 1 | bytes 8 | tf_op jit(solution)/shard_map/psum | solution.py:21
  738.7 9.5 %psum.381 = f32[]{:T(128)} all-reduce(f32[]{:T(128)} %psum.380), channel_id=1, replica_groups=mesh['asc_0'=4,'asc_1'=4,'desc_0'=4,'desc_1'=2] {'asc_1'}, use_global_device_ids=true, to_apply=%region_87.88 | all-reduce | flops 1 | bytes 8 | tf_op jit(solution)/shard_map/psum | solution.py:21
  748.2 11.3 %psum.382 = f32[]{:T(128)} all-reduce(f32[]{:T(128)} %psum.381), channel_id=1, replica_groups=mesh['asc_0'=4,'asc_1'=4,'desc_0'=4,'desc_1'=2] {'desc_0'}, use_global_device_ids=true, to_apply=%region_88.89 | all-reduce | flops 1 | bytes 8 | tf_op jit(solution)/shard_map/psum | solution.py:21
  (307 shorter events, 311.0 us)
Async XLA Ops:
  3.1 11.0 %all-to-all-start = ((f32[128,16,8]{0,1,2:T(8,128)}), f32[128,16,8]{0,1,2:T(8,128)S(1)}, u32[]{:S(2)}, u32[]{:S(2)}) async-start(f32[128,16,8]{0,1,2:T(8,128)} %copy.200), calls=%async_computation | async-start | bytes 131072 | tf_op jit(solution)/shard_map/all_to_all | solution.py:32
  14.2 14.7 %all-to-all-start.2 = ((f32[128,8,16]{0,1,2:T(8,128)}), f32[128,8,16]{0,1,2:T(8,128)S(1)}, u32[]{:S(2)}, u32[]{:S(2)}) async-start(f32[128,8,16]{0,1,2:T(8,128)} %copy.209), calls=%async_computation.2 | async-start | bytes 131072 | tf_op jit(solution)/shard_map/all_to_all | solution.py:32
  29.2 17.6 %copy-start.10 = (f32[32,128]{1,0:T(8,128)S(1)}, f32[32,128]{1,0:T(8,128)}, u32[]{:S(2)}) copy-start(f32[32,128]{1,0:T(8,128)} %param.8) | copy-start | bytes 49156
  44.9 1.3 copy-start.2
  44.9 2.0 copy-start.5
  46.9 7.0 copy-start.9
  50.3 8.7 %all-to-all-start.1 = ((f32[8,1,1024]{2,1,0:T(1,128)}), f32[8,1,1024]{2,1,0:T(1,128)S(1)}, u32[]{:S(2)}, u32[]{:S(2)}) async-start(f32[8,1,1024]{2,1,0:T(1,128)} %reshape.248), calls=%async_computation.1 | async-start | bytes 65536 | tf_op jit(solution)/shard_map/all_to_all | solution.py:118
  53.9 8.6 %copy-start.8 = (f32[64,128]{1,0:T(8,128)S(1)}, f32[64,128]{1,0:T(8,128)}, u32[]{:S(2)}) copy-start(f32[64,128]{1,0:T(8,128)} %param.14) | copy-start | bytes 98308
  53.9 16.9 %copy-start.11 = (s32[64]{0:T(128)S(1)}, s32[64]{0:T(128)}, u32[]{:S(2)}) copy-start(s32[64]{0:T(128)} %param.15) | copy-start | bytes 772
  59.0 11.0 %all-to-all-start.3 = ((f32[16,1,512]{2,1,0:T(1,128)}), f32[16,1,512]{2,1,0:T(1,128)S(1)}, u32[]{:S(2)}, u32[]{:S(2)}) async-start(f32[16,1,512]{2,1,0:T(1,128)} %reshape.246), calls=%async_computation.3 | async-start | bytes 65536 | tf_op jit(solution)/shard_map/all_to_all | solution.py:125
  71.6 9.7 %all-to-all-start.4 = ((f32[8,1,1024]{2,1,0:T(1,128)}), f32[8,1,1024]{2,1,0:T(1,128)S(1)}, u32[]{:S(2)}, u32[]{:S(2)}) async-start(f32[8,1,1024]{2,1,0:T(1,128)} %reshape.250), calls=%async_computation.4 | async-start | bytes 65536 | tf_op jit(solution)/shard_map/all_to_all | solution.py:133
  81.3 13.9 %all-to-all-start.5 = ((f32[16,1,512]{2,1,0:T(1,128)}), f32[16,1,512]{2,1,0:T(1,128)S(1)}, u32[]{:S(2)}, u32[]{:S(2)}) async-start(f32[16,1,512]{2,1,0:T(1,128)} %reshape.252), calls=%async_computation.5 | async-start | bytes 65536 | tf_op jit(solution)/shard_map/all_to_all | solution.py:140
  86.3 5.5 copy-start.3
  86.3 5.5 copy-start.6
  95.2 12.3 %all-to-all-start.6 = ((f32[8,1,1024]{2,1,0:T(1,128)}), f32[8,1,1024]{2,1,0:T(1,128)S(1)}, u32[]{:S(2)}, u32[]{:S(2)}) async-start(f32[8,1,1024]{2,1,0:T(1,128)} %reshape.256), calls=%async_computation.6 | async-start | bytes 65536 | tf_op jit(solution)/shard_map/all_to_all | solution.py:118
  99.7 4.9 copy-start
  107.6 14.9 %all-to-all-start.7 = ((f32[16,1,512]{2,1,0:T(1,128)}), f32[16,1,512]{2,1,0:T(1,128)S(1)}, u32[]{:S(2)}, u32[]{:S(2)}) async-start(f32[16,1,512]{2,1,0:T(1,128)} %reshape.254), calls=%async_computation.7 | async-start | bytes 65536 | tf_op jit(solution)/shard_map/all_to_all | solution.py:125
  124.7 42.3 %all-to-all-start.8 = ((f32[8,1,1024]{2,1,0:T(1,128)}), f32[8,1,1024]{2,1,0:T(1,128)S(1)}, u32[]{:S(2)}, u32[]{:S(2)}) async-start(f32[8,1,1024]{2,1,0:T(1,128)} %reshape.258), calls=%async_computation.8 | async-start | bytes 65536 | tf_op jit(solution)/shard_map/all_to_all | solution.py:133
  166.9 11.2 %all-to-all-start.9 = ((f32[16,1,512]{2,1,0:T(1,128)}), f32[16,1,512]{2,1,0:T(1,128)S(1)}, u32[]{:S(2)}, u32[]{:S(2)}) async-start(f32[16,1,512]{2,1,0:T(1,128)} %reshape.260), calls=%async_computation.9 | async-start | bytes 65536 | tf_op jit(solution)/shard_map/all_to_all | solution.py:140
  226.5 8.7 %all-to-all-start.10 = ((f32[8,1,1024]{2,1,0:T(1,128)}), f32[8,1,1024]{2,1,0:T(1,128)S(1)}, u32[]{:S(2)}, u32[]{:S(2)}) async-start(f32[8,1,1024]{2,1,0:T(1,128)} %reshape.264), calls=%async_computation.10 | async-start | bytes 65536 | tf_op jit(solution)/shard_map/all_to_all | solution.py:118
  235.2 11.0 %all-to-all-start.11 = ((f32[16,1,512]{2,1,0:T(1,128)}), f32[16,1,512]{2,1,0:T(1,128)S(1)}, u32[]{:S(2)}, u32[]{:S(2)}) async-start(f32[16,1,512]{2,1,0:T(1,128)} %reshape.262), calls=%async_computation.11 | async-start | bytes 65536 | tf_op jit(solution)/shard_map/all_to_all | solution.py:125
  248.5 41.4 %all-to-all-start.12 = ((f32[8,1,1024]{2,1,0:T(1,128)}), f32[8,1,1024]{2,1,0:T(1,128)S(1)}, u32[]{:S(2)}, u32[]{:S(2)}) async-start(f32[8,1,1024]{2,1,0:T(1,128)} %reshape.266), calls=%async_computation.12 | async-start | bytes 65536 | tf_op jit(solution)/shard_map/all_to_all | solution.py:133
  289.9 11.4 %all-to-all-start.13 = ((f32[16,1,512]{2,1,0:T(1,128)}), f32[16,1,512]{2,1,0:T(1,128)S(1)}, u32[]{:S(2)}, u32[]{:S(2)}) async-start(f32[16,1,512]{2,1,0:T(1,128)} %reshape.268), calls=%async_computation.13 | async-start | bytes 65536 | tf_op jit(solution)/shard_map/all_to_all | solution.py:140
  348.2 8.7 %all-to-all-start.14 = ((f32[8,1,1024]{2,1,0:T(1,128)}), f32[8,1,1024]{2,1,0:T(1,128)S(1)}, u32[]{:S(2)}, u32[]{:S(2)}) async-start(f32[8,1,1024]{2,1,0:T(1,128)} %reshape.272), calls=%async_computation.14 | async-start | bytes 65536 | tf_op jit(solution)/shard_map/all_to_all | solution.py:118
  356.9 11.0 %all-to-all-start.15 = ((f32[16,1,512]{2,1,0:T(1,128)}), f32[16,1,512]{2,1,0:T(1,128)S(1)}, u32[]{:S(2)}, u32[]{:S(2)}) async-start(f32[16,1,512]{2,1,0:T(1,128)} %reshape.270), calls=%async_computation.15 | async-start | bytes 65536 | tf_op jit(solution)/shard_map/all_to_all | solution.py:125
  410.1 8.7 %all-to-all-start.16 = ((f32[8,1,1024]{2,1,0:T(1,128)}), f32[8,1,1024]{2,1,0:T(1,128)S(1)}, u32[]{:S(2)}, u32[]{:S(2)}) async-start(f32[8,1,1024]{2,1,0:T(1,128)} %reshape.276), calls=%async_computation.16 | async-start | bytes 65536 | tf_op jit(solution)/shard_map/all_to_all | solution.py:118
  418.8 11.0 %all-to-all-start.17 = ((f32[16,1,512]{2,1,0:T(1,128)}), f32[16,1,512]{2,1,0:T(1,128)S(1)}, u32[]{:S(2)}, u32[]{:S(2)}) async-start(f32[16,1,512]{2,1,0:T(1,128)} %reshape.274), calls=%async_computation.17 | async-start | bytes 65536 | tf_op jit(solution)/shard_map/all_to_all | solution.py:125
  431.5 9.3 %all-to-all-start.18 = ((f32[8,1,1024]{2,1,0:T(1,128)}), f32[8,1,1024]{2,1,0:T(1,128)S(1)}, u32[]{:S(2)}, u32[]{:S(2)}) async-start(f32[8,1,1024]{2,1,0:T(1,128)} %reshape.278), calls=%async_computation.18 | async-start | bytes 65536 | tf_op jit(solution)/shard_map/all_to_all | solution.py:133
  440.8 13.7 %all-to-all-start.19 = ((f32[16,1,512]{2,1,0:T(1,128)}), f32[16,1,512]{2,1,0:T(1,128)S(1)}, u32[]{:S(2)}, u32[]{:S(2)}) async-start(f32[16,1,512]{2,1,0:T(1,128)} %reshape.280), calls=%async_computation.19 | async-start | bytes 65536 | tf_op jit(solution)/shard_map/all_to_all | solution.py:140
  445.7 5.5 copy-start.4
  445.7 5.5 copy-start.7
  454.6 12.6 %all-to-all-start.20 = ((f32[8,1,1024]{2,1,0:T(1,128)}), f32[8,1,1024]{2,1,0:T(1,128)S(1)}, u32[]{:S(2)}, u32[]{:S(2)}) async-start(f32[8,1,1024]{2,1,0:T(1,128)} %reshape.284), calls=%async_computation.20 | async-start | bytes 65536 | tf_op jit(solution)/shard_map/all_to_all | solution.py:118
  459.2 4.9 copy-start.1
  467.1 14.8 %all-to-all-start.21 = ((f32[16,1,512]{2,1,0:T(1,128)}), f32[16,1,512]{2,1,0:T(1,128)S(1)}, u32[]{:S(2)}, u32[]{:S(2)}) async-start(f32[16,1,512]{2,1,0:T(1,128)} %reshape.282), calls=%async_computation.21 | async-start | bytes 65536 | tf_op jit(solution)/shard_map/all_to_all | solution.py:125
  484.1 42.3 %all-to-all-start.22 = ((f32[8,1,1024]{2,1,0:T(1,128)}), f32[8,1,1024]{2,1,0:T(1,128)S(1)}, u32[]{:S(2)}, u32[]{:S(2)}) async-start(f32[8,1,1024]{2,1,0:T(1,128)} %reshape.286), calls=%async_computation.22 | async-start | bytes 65536 | tf_op jit(solution)/shard_map/all_to_all | solution.py:133
  526.4 11.0 %all-to-all-start.23 = ((f32[16,1,512]{2,1,0:T(1,128)}), f32[16,1,512]{2,1,0:T(1,128)S(1)}, u32[]{:S(2)}, u32[]{:S(2)}) async-start(f32[16,1,512]{2,1,0:T(1,128)} %reshape.288), calls=%async_computation.23 | async-start | bytes 65536 | tf_op jit(solution)/shard_map/all_to_all | solution.py:140
  586.1 8.7 %all-to-all-start.24 = ((f32[8,1,1024]{2,1,0:T(1,128)}), f32[8,1,1024]{2,1,0:T(1,128)S(1)}, u32[]{:S(2)}, u32[]{:S(2)}) async-start(f32[8,1,1024]{2,1,0:T(1,128)} %reshape.292), calls=%async_computation.24 | async-start | bytes 65536 | tf_op jit(solution)/shard_map/all_to_all | solution.py:118
  594.8 11.0 %all-to-all-start.25 = ((f32[16,1,512]{2,1,0:T(1,128)}), f32[16,1,512]{2,1,0:T(1,128)S(1)}, u32[]{:S(2)}, u32[]{:S(2)}) async-start(f32[16,1,512]{2,1,0:T(1,128)} %reshape.290), calls=%async_computation.25 | async-start | bytes 65536 | tf_op jit(solution)/shard_map/all_to_all | solution.py:125
  608.1 41.4 %all-to-all-start.26 = ((f32[8,1,1024]{2,1,0:T(1,128)}), f32[8,1,1024]{2,1,0:T(1,128)S(1)}, u32[]{:S(2)}, u32[]{:S(2)}) async-start(f32[8,1,1024]{2,1,0:T(1,128)} %reshape.294), calls=%async_computation.26 | async-start | bytes 65536 | tf_op jit(solution)/shard_map/all_to_all | solution.py:133
  649.5 11.0 %all-to-all-start.27 = ((f32[16,1,512]{2,1,0:T(1,128)}), f32[16,1,512]{2,1,0:T(1,128)S(1)}, u32[]{:S(2)}, u32[]{:S(2)}) async-start(f32[16,1,512]{2,1,0:T(1,128)} %reshape.296), calls=%async_computation.27 | async-start | bytes 65536 | tf_op jit(solution)/shard_map/all_to_all | solution.py:140
  707.4 8.7 %all-to-all-start.28 = ((f32[8,1,1024]{2,1,0:T(1,128)}), f32[8,1,1024]{2,1,0:T(1,128)S(1)}, u32[]{:S(2)}, u32[]{:S(2)}) async-start(f32[8,1,1024]{2,1,0:T(1,128)} %reshape.300), calls=%async_computation.28 | async-start | bytes 65536 | tf_op jit(solution)/shard_map/all_to_all | solution.py:118
  716.1 11.0 %all-to-all-start.29 = ((f32[16,1,512]{2,1,0:T(1,128)}), f32[16,1,512]{2,1,0:T(1,128)S(1)}, u32[]{:S(2)}, u32[]{:S(2)}) async-start(f32[16,1,512]{2,1,0:T(1,128)} %reshape.298), calls=%async_computation.29 | async-start | bytes 65536 | tf_op jit(solution)/shard_map/all_to_all | solution.py:125
where the time goes:
time: 779 us; the launch traced here: 765 us
  blocking collectives  334 us (43%)
  starting transfers between devices  122 us (16%)
  matrix products  113 us (15%)
  waiting for transfers between devices  76 us (10%)
  other arithmetic  46.6 us (6%)
  local copies, waits for them, and re-layouts  42.7 us (5%)
  between operations  31.5 us (4%)
    psum x40, blocking collectives, by_axis(): return functools.reduce(lax.psum, axes, shard)  334 us
    dot_general x12, matrix products, collect_rows(): lax.dot_general(selector, terms, (((0,), (0,)), ((), ())), precision=lax....  60.4 us
    dot_general x16, matrix products, pick_rows(): jnp.dot(selector, field, precision=lax.Precision.HIGHEST, preferred_eleme...  52.6 us
    all_to_all x8, waiting for transfers between devices, crossing(): lax.all_to_all(value_desc.reshape(blocks, cols_desc, count_asc), ASC, spl...  49.5 us
    all_to_all x8, starting transfers between devices, crossing(): lax.all_to_all(value_desc.reshape(blocks, cols_desc, count_asc), ASC, spl...  35.4 us
    unnamed x85, local copies, waits for them, and re-layouts  27.5 us
    all_to_all x8, starting transfers between devices, crossing(): lax.all_to_all(value_asc.reshape(blocks, cols_asc, count_desc), DESC, spl...  26.9 us
    all_to_all x6, starting transfers between devices, crossing(): lax.all_to_all(weighted.reshape(blocks, cols_asc, count_desc), DESC, spli...  25.4 us
  transfers between devices with their start and end apart: 30, of which 22 were waited for; matrix products, arithmetic and copies ran while one was open for 14% of the time, Pallas kernels for 0%

commit v1 on v0

v1 whole, which is shorter than its diff:
```python
import functools

import jax
import jax.numpy as jnp
import numpy as np
from jax import lax
from jax.experimental import pallas as pl
from jax.experimental.pallas import tpu as pltpu
from jax.sharding import PartitionSpec as P

MESH = pl.DeviceIdType.MESH
F32 = jnp.float32
BF16 = jnp.bfloat16
DAMPING = 2.0
INV_CAUCHY = 1.0 / 2.25
SLOTS = 16
HALF_PI_TERMS_SIN = [np.pi**n * s / f for n, s, f in ((1, 1, 1), (3, -1, 6), (5, 1, 120), (7, -1, 5040), (9, 1, 362880), (11, -1, 39916800))]
HALF_PI_TERMS_COS = [np.pi**n * s / f for n, s, f in ((0, 1, 1), (2, -1, 2), (4, 1, 24), (6, -1, 720), (8, 1, 40320), (10, -1, 3628800))]


def bits_of(p, q):
    y, x, z, c = p // 4, p % 4, q // 2, q % 2
    return (y // 2, x // 2, z // 2), (y % 2, x % 2, z % 2, c)


def cube_of(j):
    return (j % 2, (j // 2) % 2, j // 4)


def device_of(cube, member):
    return ((2 * cube[0] + member[0]) * 4 + 2 * cube[1] + member[1], (2 * cube[2] + member[2]) * 2 + member[3])


def asc_home(j, p):
    cube = cube_of(j)
    e = (p // 4 + 3 - 2 * cube[0] + 4) % 4
    f = (p % 4 + 3 - 2 * cube[1] + 4) % 4
    return cube, (e % 2, f % 2, e // 2, f // 2)


def asc_block(cube, member):
    y = (2 * cube[0] + member[0] + 1 + 2 * member[2]) % 4
    x = (2 * cube[1] + member[1] + 1 + 2 * member[3]) % 4
    return y * 4 + x


def desc_home(j, h, q):
    cube = cube_of(j)
    e = (q // 2 + 3 - 2 * cube[2] + 4) % 4
    return cube, ((h + cube[0] + cube[2]) % 2, e // 2, e % 2, q % 2)


def desc_block(cube, member):
    z = (2 * cube[2] + member[2] + 1 + 2 * member[1]) % 4
    h = (member[0] + cube[0] + cube[2]) % 2
    return h, z * 2 + member[3]


def slot_between(first, second):
    d = [(a + b) % 2 for a, b in zip(first, second)]
    return 8 * d[0] + 4 * d[1] + 2 * d[2] + d[3]


def partner(cube, member, r):
    d = (r // 8 % 2, r // 4 % 2, r // 2 % 2, r % 2)
    return device_of(cube, tuple((m + b) % 2 for m, b in zip(member, d)))


def turn(x):
    quarter = jnp.floor(2.0 * x + 0.5)
    f = x - 0.5 * quarter
    f2 = f * f
    s = jnp.full_like(f, HALF_PI_TERMS_SIN[-1])
    for term in HALF_PI_TERMS_SIN[-2::-1]:
        s = s * f2 + np.float32(term)
    s = s * f
    c = jnp.full_like(f, HALF_PI_TERMS_COS[-1])
    for term in HALF_PI_TERMS_COS[-2::-1]:
        c = c * f2 + np.float32(term)
    half = jnp.floor(0.5 * quarter)
    odd = quarter - 2.0 * half
    sign = 1.0 - 2.0 * (half - 2.0 * jnp.floor(0.5 * half))
    is_odd = odd > 0.5
    return sign * jnp.where(is_odd, -s, c), sign * jnp.where(is_odd, c, s)


def times(a, b):
    return a[0] * b[0] - a[1] * b[1], a[0] * b[1] + a[1] * b[0]


def split(value):
    high = value.astype(BF16)
    return high, (value - high.astype(F32)).astype(BF16)


def fold(value):
    return jnp.sum(value, axis=0, keepdims=True)


def kernel(
    coef_a, coef_d, ids_a, ids_d, time_a, time_d, height, fill,
    out_a, out_d,
    turned, stage_a, stage_d, got_a, got_d, coefs,
    basis_a, basis_d, mine_a, mine_d, theirs_a, theirs_d,
    weight_a, weight_d, err_a, err_d, y_a, y_d, vecs,
    part, ring_z, part_z, ring_xy, home_a, home_d,
    init_sem_a, init_sem_d, init_send, coef_sem, coef_send,
    swap_sem, swap_send, sum_sem, sum_send, home_sem, home_send,
):
    p, q = lax.axis_index("asc"), lax.axis_index("desc")
    cube, member = bits_of(p, q)
    me_class = 4 * cube[2] + 2 * cube[1] + cube[0]
    my_asc = asc_block(cube, member)
    my_h, my_q = desc_block(cube, member)
    my_i = me_class + 8 * my_h

    def at(cube_member):
        return device_of(*cube_member)

    barrier = pltpu.get_barrier_semaphore()

    def greet(device):
        pl.semaphore_signal(barrier, inc=1, device_id=device, device_id_type=MESH)

    def greet_column(k, carry):
        greet((my_asc, k))
        return carry

    def greet_row(k, carry):
        greet((k, my_q))
        return carry

    def greet_cube(k, carry):
        greet(partner(cube, member, k))
        return carry

    def greet_z(k, carry):
        greet((p, (q + k) % 8))
        return carry

    def greet_xy(k, carry):
        greet(((p + k) % 16, q))
        return carry

    lax.fori_loop(0, 8, greet_column, 0)
    lax.fori_loop(0, 16, greet_row, 0)
    lax.fori_loop(1, 16, greet_cube, 0)
    lax.fori_loop(1, 8, greet_z, 0)
    lax.fori_loop(1, 16, greet_xy, 0)
    greet(at(asc_home(q, p)))
    greet(at(desc_home(p % 8, p // 8, q)))

    row = lax.broadcasted_iota(jnp.int32, (64, 128), 0)
    lane = lax.broadcasted_iota(jnp.int32, (64, 128), 1)
    fill_row = fill[...].astype(F32)
    fills = jnp.concatenate([fill_row, fill_row], axis=1)
    slot = (row + 64 * (lane // 64)).astype(F32)
    live = slot < fills
    sources = (
        (ids_a[...] % 32).astype(F32),
        time_a[...],
        height[...],
        (ids_d[...] % 32).astype(F32),
        time_d[...],
    )
    for k, source in enumerate(sources):
        both = jnp.concatenate([source, pltpu.roll(source, 64, 1)], axis=0)
        flat = both.T[0:64]
        turned[k] = jnp.where(live, flat, -1.0) if k in (0, 3) else flat
    for i in range(16):
        for k in range(3):
            stage_a[i, k] = turned[k, pl.ds(i, 4, stride=16), :]
        for k in range(2):
            stage_d[i, k] = turned[3 + k, pl.ds(i, 4, stride=16), :]

    pl.semaphore_wait(barrier, 8 + 16 + 15 + 7 + 15 + 2)

    def coef_copy(side, source, device):
        return pltpu.make_async_remote_copy(
            src_ref=source, dst_ref=coefs.at[side], send_sem=coef_send.at[side], recv_sem=coef_sem.at[side],
            device_id=device, device_id_type=MESH,
        )

    send_coef_a = coef_copy(0, coef_a, at(asc_home(q, p)))
    send_coef_d = coef_copy(1, coef_d, at(desc_home(p % 8, p // 8, q)))
    send_coef_a.start()
    send_coef_d.start()

    def send_slots(i, carry):
        j, h = i % 8, i // 8
        a_home, d_home = asc_home(j, p), desc_home(j, h, q)
        r = slot_between(a_home[1], d_home[1])
        pltpu.make_async_remote_copy(
            src_ref=stage_a.at[i], dst_ref=got_a.at[r], send_sem=init_send.at[0], recv_sem=init_sem_a.at[r],
            device_id=at(a_home), device_id_type=MESH,
        ).start()
        pltpu.make_async_remote_copy(
            src_ref=stage_d.at[i], dst_ref=got_d.at[r], send_sem=init_send.at[1], recv_sem=init_sem_d.at[r],
            device_id=at(d_home), device_id_type=MESH,
        ).start()
        return carry

    lax.fori_loop(0, 16, send_slots, 0)

    frequency = (lax.broadcasted_iota(jnp.int32, (8, 128), 0) + 1).astype(F32)
    arc = lax.broadcasted_iota(jnp.int32, (32, 128), 0).astype(F32)

    def make_basis(r, got, basis):
        for l in range(4):
            t = jnp.broadcast_to(got[r, 1, l : l + 1, :], (8, 128))
            first = turn(frequency * t)
            e8 = tuple(jnp.broadcast_to(v[7:8], (8, 128)) for v in first)
            e16 = times(e8, e8)
            e32 = times(e16, e16)
            blocks = [first, times(first, e8)]
            blocks += [times(b, e16) for b in blocks]
            blocks += [times(b, e32) for b in blocks]
            terms = jnp.concatenate([b[0] for b in blocks] + [b[1] for b in blocks], axis=0)
            high, low = split(terms)
            basis[r, 0:128, 128 * l : 128 * (l + 1)] = high
            basis[r, 128:256, 128 * l : 128 * (l + 1)] = low

    def left_of(vector):
        high, low = split(vector)
        return jnp.concatenate(
            [jnp.concatenate([high, high], axis=1), jnp.concatenate([low, low], axis=1)], axis=0
        )

    def apply(r, left, got, basis, mine, par, take_height):
        terms = jnp.dot(left, basis[r], preferred_element_type=F32)
        terms = terms[0:32] + terms[32:64]
        for l in range(4):
            ids = jnp.broadcast_to(got[r, 0, l : l + 1, :], (32, 128))
            line = fold(jnp.where(ids == arc, terms[:, 128 * l : 128 * (l + 1)], 0.0))
            if take_height:
                line = line - got[r, 2, l : l + 1, :]
            mine[par, r, l : l + 1, :] = line

    def swap(par, r):
        device = partner(cube, member, r)
        return (
            pltpu.make_async_remote_copy(
                src_ref=mine_a.at[par, r], dst_ref=theirs_d.at[par, r],
                send_sem=swap_send.at[par, 0], recv_sem=swap_sem.at[par, 1, r],
                device_id=device, device_id_type=MESH,
            ),
            pltpu.make_async_remote_copy(
                src_ref=mine_d.at[par, r], dst_ref=theirs_a.at[par, r],
                send_sem=swap_send.at[par, 1], recv_sem=swap_sem.at[par, 0, r],
                device_id=device, device_id_type=MESH,
            ),
        )

    def forward(par, vector, build):
        left_a, left_d = left_of(vector[0:32]), left_of(vector[32:64])

        def one(r):
            if build:
                pltpu.make_async_copy(got_a.at[r], got_a.at[r], init_sem_a.at[r]).wait()
                pltpu.make_async_copy(got_d.at[r], got_d.at[r], init_sem_d.at[r]).wait()
                make_basis(r, got_a, basis_a)
                make_basis(r, got_d, basis_d)
            apply(r, left_a, got_a, basis_a, mine_a, par, build)
            apply(r, left_d, got_d, basis_d, mine_d, par, False)

        def step(k, carry):
            r = 15 - k
            one(r)
            for copy in swap(par, r):
                copy.start()
            return carry

        lax.fori_loop(0, 15, step, 0)
        one(0)
        theirs_a[par, 0] = mine_d[par, 0]
        theirs_d[par, 0] = mine_a[par, 0]

    def collect(par, r, z, got):
        high, low = split(z)
        lines = []
        for l in range(4):
            ids = jnp.broadcast_to(got[r, 0, l : l + 1, :], (32, 128))
            hit = ids == arc
            zs = jnp.broadcast_to(z[l : l + 1], (32, 128))
            zh, zl = split(jnp.where(hit, zs, 0.0))
            lines.append(jnp.concatenate([zh, zl], axis=0))
        return jnp.concatenate(lines, axis=1)

    def contract(placed, basis):
        return lax.dot_general(placed, basis, (((1,), (1,)), ((), ())), preferred_element_type=F32)

    def unfold(total):
        return total[0:32, 0:128] + (total[0:32, 128:256] + total[32:64, 0:128]) + total[32:64, 128:256]

    def backward(par, react):
        def one(r, carry):
            total_a, total_d = carry
            z_a, z_d = react(r)
            total_a += contract(collect(par, r, z_a, got_a), basis_a[r])
            total_d += contract(collect(par, r, z_d, got_d), basis_d[r])
            return total_a, total_d

        def step(r, carry):
            pltpu.make_async_copy(theirs_a.at[par, r], theirs_a.at[par, r], swap_sem.at[par, 0, r]).wait()
            pltpu.make_async_copy(theirs_d.at[par, r], theirs_d.at[par, r], swap_sem.at[par, 1, r]).wait()
            return one(r, carry)

        zero = jnp.zeros((64, 256), F32)
        total_a, total_d = lax.fori_loop(1, 16, step, one(0, (zero, zero)))
        wait_sent(par)
        return jnp.concatenate([unfold(total_a), unfold(total_d)], axis=0)

    def wait_sent(par):
        for k, mine in enumerate((mine_a, mine_d)):
            sent = mine.at[par, pl.ds(1, 15)]
            pltpu.make_async_copy(sent, sent, swap_send.at[par, k]).wait()

    def misfit(par, first):
        def react(r):
            if first:
                err_a[r] = mine_a[par, r] - theirs_a[par, r]
                err_d[r] = theirs_d[par, r] - mine_d[par, r]
            zs = []
            for err, got, weight in ((err_a, got_a, weight_a), (err_d, got_d, weight_d)):
                lives = jnp.where(got[r, 0] >= 0.0, 1.0, 0.0)
                m = -lives * err[r]
                w = lives / (1.0 + m * m * INV_CAUCHY)
                weight[r] = w
                zs.append(w * m)
            return zs[0], -zs[1]

        return react

    def image(par, n):
        def react(r):
            a = mine_a[par, r] - theirs_a[par, r]
            d = theirs_d[par, r] - mine_d[par, r]
            y_a[n, r] = a
            y_d[n, r] = d
            return weight_a[r] * a, -(weight_d[r] * d)

        return react

    def take(par, n):
        def step(r, carry):
            pltpu.make_async_copy(theirs_a.at[par, r], theirs_a.at[par, r], swap_sem.at[par, 0, r]).wait()
            pltpu.make_async_copy(theirs_d.at[par, r], theirs_d.at[par, r], swap_sem.at[par, 1, r]).wait()
            return carry

        lax.fori_loop(1, 16, step, 0)
        wait_sent(par)
        y_a[n] = mine_a[par] - theirs_a[par]
        y_d[n] = theirs_d[par] - mine_d[par]

    def sum_first(n, rows):
        rows = rows + [jnp.zeros((1, 128), F32)] * (8 - len(rows))
        part[n] = jnp.concatenate(rows, axis=0)

        def send(k, carry):
            pltpu.make_async_remote_copy(
                src_ref=part.at[n], dst_ref=ring_z.at[n, k], send_sem=sum_send.at[n, 0], recv_sem=sum_sem.at[n, 0],
                device_id=(p, (q + 8 - k) % 8), device_id_type=MESH,
            ).start()
            return carry

        lax.fori_loop(1, 8, send, 0)
        ring_z[n, 0] = part[n]

    def sum_second(n):
        whole = ring_z.at[n, pl.ds(1, 7)]
        pltpu.make_async_copy(whole, whole, sum_sem.at[n, 0]).wait()
        total = ring_z[n, (8 - q) % 8]
        for k in range(1, 8):
            total = total + ring_z[n, (k + 8 - q) % 8]
        part_z[n] = total

        def send(k, carry):
            pltpu.make_async_remote_copy(
                src_ref=part_z.at[n], dst_ref=ring_xy.at[n, k], send_sem=sum_send.at[n, 1], recv_sem=sum_sem.at[n, 1],
                device_id=((p + 16 - k) % 16, q), device_id_type=MESH,
            ).start()
            return carry

        lax.fori_loop(1, 16, send, 0)
        ring_xy[n, 0] = total

    def sum_last(n):
        whole = ring_xy.at[n, pl.ds(1, 15)]
        pltpu.make_async_copy(whole, whole, sum_sem.at[n, 1]).wait()
        total = ring_xy[n, (16 - p) % 16]
        for k in range(1, 16):
            total = total + ring_xy[n, (k + 16 - p) % 16]
        pltpu.make_async_copy(ring_z.at[n, pl.ds(1, 7)], ring_z.at[n, pl.ds(1, 7)], sum_send.at[n, 0]).wait()
        pltpu.make_async_copy(whole, whole, sum_send.at[n, 1]).wait()
        total = jnp.sum(total, axis=1, keepdims=True)
        return [total[k : k + 1, 0:1] for k in range(8)]

    def send_home(k):
        for side, buffer, device in ((0, home_a, (my_asc, me_class)), (1, home_d, (my_i, my_q))):
            pltpu.make_async_remote_copy(
                src_ref=vecs.at[k, pl.ds(32 * side, 32)], dst_ref=buffer.at[k],
                send_sem=home_send.at[side, k], recv_sem=home_sem.at[side, k],
                device_id=device, device_id_type=MESH,
            ).start()

    send_coef_a.wait_recv()
    send_coef_d.wait_recv()
    state = jnp.concatenate([coefs[0], coefs[1]], axis=0)
    par = 0
    forward(par, state, True)
    for step in range(2):
        last = step == 1
        if step == 0:
            gradient = backward(par, misfit(par, True))
            par = 1 - par
        else:
            react = misfit(par, False)

            def gather(r, carry):
                z_a, z_d = react(r)
                return (
                    carry[0] + contract(collect(0, r, z_a, got_a), basis_a[r]),
                    carry[1] + contract(collect(0, r, z_d, got_d), basis_d[r]),
                )

            zero = jnp.zeros((64, 256), F32)
            total_a, total_d = lax.fori_loop(0, 16, gather, (zero, zero))
            gradient = jnp.concatenate([unfold(total_a), unfold(total_d)], axis=0)
        r0 = gradient - DAMPING * state
        vecs[0] = state
        vecs[1] = r0
        forward(par, r0, False)
        if last:
            send_home(0)
            send_home(1)
        v1 = backward(par, image(par, 0)) + DAMPING * r0
        par = 1 - par
        vecs[2] = v1
        sum_first(2 * step, [fold(r0 * r0), fold(r0 * v1)])
        forward(par, v1, False)
        if last:
            send_home(2)
        sum_second(2 * step)
        v2 = backward(par, image(par, 1)) + DAMPING * v1
        par = 1 - par
        vecs[3] = v2
        forward(par, v2, False)
        if last:
            send_home(3)
        rr0, mu0 = sum_last(2 * step)[0:2]
        a0 = rr0 / mu0
        r1 = r0 - a0 * v1
        u1 = v1 - a0 * v2
        take(par, 2)
        par = 1 - par
        ju = y_a[1] - a0 * y_a[2]
        curve = jnp.sum(weight_a[...] * ju * ju, axis=0)
        sum_first(
            2 * step + 1,
            [fold(r1 * r1), fold(r1 * u1), fold(r1 * v1), fold(u1 * u1), fold(u1 * v1), fold(v1 * v1), fold(curve)],
        )
        sum_second(2 * step + 1)
        rr1, ru, rv, uu, uv, vv, wuu = sum_last(2 * step + 1)[0:7]
        b1 = rr1 / rr0
        a1 = rr1 / (ru + 2.0 * b1 * rv + b1 * b1 * mu0)
        g1 = a1 * b1
        rr2 = rr1 + a1 * a1 * uu + g1 * g1 * vv - 2.0 * a1 * ru - 2.0 * g1 * rv + 2.0 * a1 * g1 * uv
        rr2 = jnp.maximum(rr2, 0.0)
        b2 = rr2 / rr1
        pr, pu, pv, p0 = 1.0 + b2, -a1, -g1, b2 * b1
        m_uu, m_uv, m_vv = wuu + 2.0 * uu, (uv - uu) / a0, (vv - uv) / a0
        curve2 = (
            pr * pr * ru + pu * pu * m_uu + pv * pv * m_vv + p0 * p0 * mu0
            + 2.0 * (pr * pu * uu + pr * pv * uv + pr * p0 * rv + pu * pv * m_uv + pu * p0 * uv + pv * p0 * vv)
        )
        a2 = rr2 / jnp.maximum(curve2, jnp.maximum(2.0 * rr2, 1e-30))
        c_r = a1 + a2 * pr
        c_u = a2 * pu
        k0 = a0 + g1 + a2 * p0 + c_r
        k1 = a2 * pv - a0 * c_r + c_u
        k2 = -a0 * c_u
        if not last:
            state = state + (k0 * r0 + k1 * v1 + k2 * v2)
            for err, y in ((err_a, y_a), (err_d, y_d)):
                err[...] = err[...] + (k0 * y[0] + k1 * y[1] + k2 * y[2])

    send_coef_a.wait_send()
    send_coef_d.wait_send()
    pltpu.make_async_copy(stage_a, stage_a, init_send.at[0]).wait()
    pltpu.make_async_copy(stage_d, stage_d, init_send.at[1]).wait()
    for side, (buffer, out) in enumerate(((home_a, out_a), (home_d, out_d))):
        for k in range(4):
            pltpu.make_async_copy(buffer.at[k], buffer.at[k], home_sem.at[side, k]).wait()
            pltpu.make_async_copy(buffer.at[k], buffer.at[k], home_send.at[side, k]).wait()
        out[...] = buffer[0] + (k0 * buffer[1] + k1 * buffer[2] + k2 * buffer[3])


def body(coef_a, coef_d, cross_a, cross_d, time_a, time_d, height, fill):
    vmem = pl.BlockSpec(memory_space=pltpu.VMEM)
    values = pltpu.VMEM((SLOTS, 4, 128), F32)
    dma = pltpu.SemaphoreType.DMA
    return pl.pallas_call(
        kernel,
        out_shape=(jax.ShapeDtypeStruct((32, 128), F32),) * 2,
        in_specs=[vmem] * 8,
        out_specs=(vmem, vmem),
        scratch_shapes=[
            pltpu.VMEM((5, 64, 128), F32),
            pltpu.VMEM((16, 3, 4, 128), F32),
            pltpu.VMEM((16, 2, 4, 128), F32),
            pltpu.VMEM((SLOTS, 3, 4, 128), F32),
            pltpu.VMEM((SLOTS, 2, 4, 128), F32),
            pltpu.VMEM((2, 32, 128), F32),
            pltpu.VMEM((SLOTS, 256, 512), BF16),
            pltpu.VMEM((SLOTS, 256, 512), BF16),
            pltpu.VMEM((2, SLOTS, 4, 128), F32),
            pltpu.VMEM((2, SLOTS, 4, 128), F32),
            pltpu.VMEM((2, SLOTS, 4, 128), F32),
            pltpu.VMEM((2, SLOTS, 4, 128), F32),
            values,
            values,
            values,
            values,
            pltpu.VMEM((3, SLOTS, 4, 128), F32),
            pltpu.VMEM((3, SLOTS, 4, 128), F32),
            pltpu.VMEM((4, 64, 128), F32),
            pltpu.VMEM((4, 8, 128), F32),
            pltpu.VMEM((4, 8, 8, 128), F32),
            pltpu.VMEM((4, 8, 128), F32),
            pltpu.VMEM((4, 16, 8, 128), F32),
            pltpu.VMEM((4, 32, 128), F32),
            pltpu.VMEM((4, 32, 128), F32),
            dma((SLOTS,)),
            dma((SLOTS,)),
            dma((2,)),
            dma((2,)),
            dma((2,)),
            dma((2, 2, SLOTS)),
            dma((2, 2)),
            dma((4, 2)),
            dma((4, 2)),
            dma((2, 4)),
            dma((2, 4)),
        ],
        compiler_params=pltpu.CompilerParams(collective_id=0, has_side_effects=True),
        name="adjust",
    )(coef_a, coef_d, cross_a, cross_d, time_a, time_d, height, fill.reshape(1, -1))


def solution(mesh):
    rows = P(("asc", "desc"), None)
    return jax.shard_map(
        body,
        mesh=mesh,
        in_specs=(rows,) * 7 + (P(("asc", "desc")),),
        out_specs=(rows, rows),
        check_vma=False,
    )
```

time: 779 us -> 106 us (0.14); the launches traced: 765 us -> 106 us
  blocking collectives: 334 us -> 0 us
  starting transfers between devices: 122 us -> 0 us
  matrix products: 113 us -> 0 us
  Pallas kernels: 0 us -> 103 us
  waiting for transfers between devices: 76 us -> 0 us
  other arithmetic: 46.6 us -> 0 us
  local copies, waits for them, and re-layouts: 42.7 us -> 1.94 us
  between operations: 31.5 us -> 0.65 us
    psum x40 -> x0, blocking collectives: 334 us -> none  [by_axis(): return functools.reduce(lax.psum, axes, shard)]
    all_to_all x30 -> x0, starting transfers between devices: 122 us -> none  [the longest x8 35.4 us: crossing(): lax.all_to_all(value_desc.reshape(blocks, cols_desc, count_asc), ASC, spl...]
    dot_general x28 -> x0, matrix products: 113 us -> none  [the longest x12 60.4 us: collect_rows(): lax.dot_general(selector, terms, (((0,), (0,)), ((), ())), precision=lax....]
    pallas_call x0 -> x1, Pallas kernels: none -> 103 us  [body(): pl.pallas_call(kernel, out_shape=(jax.ShapeDtypeStruct((32, 128), F32),)...]
    all_to_all x30 -> x0, waiting for transfers between devices: 76 us -> none  [the longest x8 49.5 us: crossing(): lax.all_to_all(value_desc.reshape(blocks, cols_desc, count_asc), ASC, spl...]
    unnamed x85 -> x4, local copies, waits for them, and re-layouts: 27.5 us -> 1.94 us
    all_to_all x28 -> x0, other arithmetic: 20.2 us -> none  [the longest x8 5.77 us: crossing(): lax.all_to_all(value_asc.reshape(blocks, cols_asc, count_desc), DESC, spl...]
    cos x1 -> x0, other arithmetic: 15.6 us -> none  [harmonics(): return jnp.concatenate([jnp.cos(phases), jnp.sin(phases)], axis=1)]
  transfers between devices with their start and end apart: 30 -> 0, of which waited for: 22 -> 0; matrix products, arithmetic and copies ran while one was open for 14% -> 0% of each run, Pallas kernels for 0% -> 0%
where the time goes in v1:
time: 106 us
  Pallas kernels  103 us (97%)
  local copies, waits for them, and re-layouts  1.94 us (2%)
    pallas_call x1, Pallas kernels, body(): pl.pallas_call(kernel, out_shape=(jax.ShapeDtypeStruct((32, 128), F32),)...  103 us

profile of v1, /device:TPU:0, one launch (start us, length us, event | category | flops | bytes accessed | tf_op | source)
XLA Modules:
  0.0 105.8 jit_solution(7375803022615970488)
XLA Ops:
  0.6 103.2 %adjust.1 = (f32[32,128]{1,0:T(8,128)}, f32[32,128]{1,0:T(8,128)}) custom-call(f32[32,128]{1,0:T(8,128)} %coef_a.1, f32[32,128]{1,0:T(8,128)} %coef_d.1, s32[64,128]{1,0:T(8,128)} %ids_a.1, s32[64,128]{1,0:T(8,128)} %ids_d.1, f32[64,128]{1,0:T(8,128)} %time_a.1, f32[64,128]{1,0:T(8,128)} %time_d.1, f32[64,128]{1,0:T(8,128)} %height.1, s32[1,64]{1,0:T(1,128)} %bitcast.1), custom_call_target="tpu_custom_call" | custom-call | tf_op jit(solution)/shard_map/adjust/pallas_call | solution.py:502
  103.9 0.0 copy-start
  103.9 1.3 %copy.12 = f32[32,128]{1,0:T(8,128)} copy(f32[32,128]{1,0:T(8,128)} %get-tuple-element.4) | data formatting | bytes 32768
  105.2 0.0 copy-done
  105.2 0.6 copy.13
Async XLA Ops:
  103.9 1.3 %copy-start = (f32[32,128]{1,0:T(8,128)S(1)}, f32[32,128]{1,0:T(8,128)}, u32[]{:S(2)}) copy-start(f32[32,128]{1,0:T(8,128)} %get-tuple-element.5) | copy-start | bytes 49156

commit v2 on v1

--- a/solution.py
+++ b/solution.py
@@ -18,13 +18,21 @@
 HALF_PI_TERMS_COS = [np.pi**n * s / f for n, s, f in ((0, 1, 1), (2, -1, 2), (4, 1, 24), (6, -1, 720), (8, 1, 40320), (10, -1, 3628800))]
 
 
+def div(a, n):
+    return a // n if isinstance(a, int) else lax.div(a, jnp.int32(n))
+
+
+def rem(a, n):
+    return a % n if isinstance(a, int) else lax.rem(a, jnp.int32(n))
+
+
 def bits_of(p, q):
-    y, x, z, c = p // 4, p % 4, q // 2, q % 2
-    return (y // 2, x // 2, z // 2), (y % 2, x % 2, z % 2, c)
+    y, x, z, c = div(p, 4), rem(p, 4), div(q, 2), rem(q, 2)
+    return (div(y, 2), div(x, 2), div(z, 2)), (rem(y, 2), rem(x, 2), rem(z, 2), c)
 
 
 def cube_of(j):
-    return (j % 2, (j // 2) % 2, j // 4)
+    return (rem(j, 2), rem(div(j, 2), 2), div(j, 4))
 
 
 def device_of(cube, member):
@@ -33,37 +41,37 @@
 
 def asc_home(j, p):
     cube = cube_of(j)
-    e = (p // 4 + 3 - 2 * cube[0] + 4) % 4
-    f = (p % 4 + 3 - 2 * cube[1] + 4) % 4
-    return cube, (e % 2, f % 2, e // 2, f // 2)
+    e = rem(div(p, 4) + 7 - 2 * cube[0], 4)
+    f = rem(rem(p, 4) + 7 - 2 * cube[1], 4)
+    return cube, (rem(e, 2), rem(f, 2), div(e, 2), div(f, 2))
 
 
 def asc_block(cube, member):
-    y = (2 * cube[0] + member[0] + 1 + 2 * member[2]) % 4
-    x = (2 * cube[1] + member[1] + 1 + 2 * member[3]) % 4
+    y = rem(2 * cube[0] + member[0] + 1 + 2 * member[2], 4)
+    x = rem(2 * cube[1] + member[1] + 1 + 2 * member[3], 4)
     return y * 4 + x
 
 
 def desc_home(j, h, q):
     cube = cube_of(j)
-    e = (q // 2 + 3 - 2 * cube[2] + 4) % 4
-    return cube, ((h + cube[0] + cube[2]) % 2, e // 2, e % 2, q % 2)
+    e = rem(div(q, 2) + 7 - 2 * cube[2], 4)
+    return cube, (rem(h + cube[0] + cube[2], 2), div(e, 2), rem(e, 2), rem(q, 2))
 
 
 def desc_block(cube, member):
-    z = (2 * cube[2] + member[2] + 1 + 2 * member[1]) % 4
-    h = (member[0] + cube[0] + cube[2]) % 2
+    z = rem(2 * cube[2] + member[2] + 1 + 2 * member[1], 4)
+    h = rem(member[0] + cube[0] + cube[2], 2)
     return h, z * 2 + member[3]
 
 
 def slot_between(first, second):
-    d = [(a + b) % 2 for a, b in zip(first, second)]
+    d = [rem(a + b, 2) for a, b in zip(first, second)]
     return 8 * d[0] + 4 * d[1] + 2 * d[2] + d[3]
 
 
-def partner(cube, member, r):
-    d = (r // 8 % 2, r // 4 % 2, r // 2 % 2, r % 2)
-    return device_of(cube, tuple((m + b) % 2 for m, b in zip(member, d)))
+def partner(cube, member, high, low):
+    d = (div(high, 2), rem(high, 2), div(low, 2), rem(low, 2))
+    return device_of(cube, tuple(m if isinstance(b, int) and b == 0 else rem(m + b, 2) for m, b in zip(member, d)))
 
 
 def turn(x):
@@ -122,33 +130,18 @@
     def greet(device):
         pl.semaphore_signal(barrier, inc=1, device_id=device, device_id_type=MESH)
 
-    def greet_column(k, carry):
-        greet((my_asc, k))
-        return carry
-
-    def greet_row(k, carry):
-        greet((k, my_q))
-        return carry
-
-    def greet_cube(k, carry):
-        greet(partner(cube, member, k))
-        return carry
-
-    def greet_z(k, carry):
-        greet((p, (q + k) % 8))
-        return carry
-
-    def greet_xy(k, carry):
-        greet(((p + k) % 16, q))
-        return carry
-
-    lax.fori_loop(0, 8, greet_column, 0)
-    lax.fori_loop(0, 16, greet_row, 0)
-    lax.fori_loop(1, 16, greet_cube, 0)
-    lax.fori_loop(1, 8, greet_z, 0)
-    lax.fori_loop(1, 16, greet_xy, 0)
+    for k in range(8):
+        greet((my_asc, rem(q + k, 8)))
+    for k in range(16):
+        greet((rem(p + k, 16), my_q))
+    for k in range(1, 16):
+        greet(partner(cube, member, k // 4, k % 4))
+    for k in range(1, 8):
+        greet((p, rem(q + k, 8)))
+    for k in range(1, 16):
+        greet((rem(p + k, 16), q))
     greet(at(asc_home(q, p)))
-    greet(at(desc_home(p % 8, p // 8, q)))
+    greet(at(desc_home(rem(p, 8), div(p, 8), q)))
 
     row = lax.broadcasted_iota(jnp.int32, (64, 128), 0)
     lane = lax.broadcasted_iota(jnp.int32, (64, 128), 1)
@@ -182,25 +175,32 @@
         )
 
     send_coef_a = coef_copy(0, coef_a, at(asc_home(q, p)))
-    send_coef_d = coef_copy(1, coef_d, at(desc_home(p % 8, p // 8, q)))
+    send_coef_d = coef_copy(1, coef_d, at(desc_home(rem(p, 8), div(p, 8), q)))
     send_coef_a.start()
     send_coef_d.start()
 
-    def send_slots(i, carry):
-        j, h = i % 8, i // 8
-        a_home, d_home = asc_home(j, p), desc_home(j, h, q)
-        r = slot_between(a_home[1], d_home[1])
-        pltpu.make_async_remote_copy(
-            src_ref=stage_a.at[i], dst_ref=got_a.at[r], send_sem=init_send.at[0], recv_sem=init_sem_a.at[r],
-            device_id=at(a_home), device_id_type=MESH,
-        ).start()
-        pltpu.make_async_remote_copy(
-            src_ref=stage_d.at[i], dst_ref=got_d.at[r], send_sem=init_send.at[1], recv_sem=init_sem_d.at[r],
-            device_id=at(d_home), device_id_type=MESH,
-        ).start()
+    def send_slots(k, carry):
+        j = rem(k + q, 8)
+        a_home = asc_home(j, p)
+        for h in range(2):
+            d_home = desc_home(j, h, q)
+            r = slot_between(a_home[1], d_home[1])
+            pltpu.make_async_remote_copy(
+                src_ref=stage_a.at[j + 8 * h], dst_ref=got_a.at[r], send_sem=init_send.at[0], recv_sem=init_sem_a.at[r],
+                device_id=at(a_home), device_id_type=MESH,
+            ).start()
+        j = rem(k + p, 8)
+        a_home = asc_home(j, p)
+        for h in range(2):
+            d_home = desc_home(j, h, q)
+            r = slot_between(a_home[1], d_home[1])
+            pltpu.make_async_remote_copy(
+                src_ref=stage_d.at[j + 8 * h], dst_ref=got_d.at[r], send_sem=init_send.at[1], recv_sem=init_sem_d.at[r],
+                device_id=at(d_home), device_id_type=MESH,
+            ).start()
         return carry
 
-    lax.fori_loop(0, 16, send_slots, 0)
+    lax.fori_loop(0, 8, send_slots, 0)
 
     frequency = (lax.broadcasted_iota(jnp.int32, (8, 128), 0) + 1).astype(F32)
     arc = lax.broadcasted_iota(jnp.int32, (32, 128), 0).astype(F32)
@@ -236,54 +236,61 @@
                 line = line - got[r, 2, l : l + 1, :]
             mine[par, r, l : l + 1, :] = line
 
-    def swap(par, r):
-        device = partner(cube, member, r)
-        return (
+    def swap(par, high, low):
+        device = partner(cube, member, high, low)
+        r = 4 * high + low
+        for mine, theirs, mine_kind in ((mine_a, theirs_d, 0), (mine_d, theirs_a, 1)):
             pltpu.make_async_remote_copy(
-                src_ref=mine_a.at[par, r], dst_ref=theirs_d.at[par, r],
-                send_sem=swap_send.at[par, 0], recv_sem=swap_sem.at[par, 1, r],
+                src_ref=mine.at[par, r], dst_ref=theirs.at[par, r],
+                send_sem=swap_send.at[par, mine_kind], recv_sem=swap_sem.at[par, 1 - mine_kind, r],
                 device_id=device, device_id_type=MESH,
-            ),
-            pltpu.make_async_remote_copy(
-                src_ref=mine_d.at[par, r], dst_ref=theirs_a.at[par, r],
-                send_sem=swap_send.at[par, 1], recv_sem=swap_sem.at[par, 0, r],
-                device_id=device, device_id_type=MESH,
-            ),
-        )
+            ).start()
+
+    def wait_swapped(par, r):
+        for k, theirs in enumerate((theirs_a, theirs_d)):
+            pltpu.make_async_copy(theirs.at[par, r], theirs.at[par, r], swap_sem.at[par, k, r]).wait()
 
     def forward(par, vector, build):
         left_a, left_d = left_of(vector[0:32]), left_of(vector[32:64])
 
-        def one(r):
+        def prepare(r):
+            pltpu.make_async_copy(got_a.at[r], got_a.at[r], init_sem_a.at[r]).wait()
+            pltpu.make_async_copy(got_d.at[r], got_d.at[r], init_sem_d.at[r]).wait()
+            make_basis(r, got_a, basis_a)
+            make_basis(r, got_d, basis_d)
+
+        def four(high):
+            for low in range(3, -1, -1):
+                r = 4 * high + low
+                apply(r, left_a, got_a, basis_a, mine_a, par, build)
+                apply(r, left_d, got_d, basis_d, mine_d, par, False)
+
+        def step(k, carry):
+            high = 3 - k
             if build:
-                pltpu.make_async_copy(got_a.at[r], got_a.at[r], init_sem_a.at[r]).wait()
-                pltpu.make_async_copy(got_d.at[r], got_d.at[r], init_sem_d.at[r]).wait()
-                make_basis(r, got_a, basis_a)
-                make_basis(r, got_d, basis_d)
-            apply(r, left_a, got_a, basis_a, mine_a, par, build)
-            apply(r, left_d, got_d, basis_d, mine_d, par, False)
-
-        def step(k, carry):
-            r = 15 - k
-            one(r)
-            for copy in swap(par, r):
-                copy.start()
+                lax.fori_loop(4 * high, 4 * high + 4, lambda r, c: (prepare(r), c)[1], 0)
+            four(high)
+            for low in range(3, -1, -1):
+                swap(par, high, low)
             return carry
 
-        lax.fori_loop(0, 15, step, 0)
-        one(0)
+        lax.fori_loop(0, 3, step, 0)
+        if build:
+            lax.fori_loop(0, 4, lambda r, c: (prepare(r), c)[1], 0)
+        four(0)
+        for low in range(3, 0, -1):
+            swap(par, 0, low)
         theirs_a[par, 0] = mine_d[par, 0]
         theirs_d[par, 0] = mine_a[par, 0]
 
     def collect(par, r, z, got):
-        high, low = split(z)
+        high = z.astype(BF16).astype(F32)
+        low = z - high
         lines = []
         for l in range(4):
-            ids = jnp.broadcast_to(got[r, 0, l : l + 1, :], (32, 128))
-            hit = ids == arc
-            zs = jnp.broadcast_to(z[l : l + 1], (32, 128))
-            zh, zl = split(jnp.where(hit, zs, 0.0))
-            lines.append(jnp.concatenate([zh, zl], axis=0))
+            hit = jnp.broadcast_to(got[r, 0, l : l + 1, :], (32, 128)) == arc
+            both = [jnp.where(hit, jnp.broadcast_to(v[l : l + 1], (32, 128)), 0.0) for v in (high, low)]
+            lines.append(jnp.concatenate(both, axis=0).astype(BF16))
         return jnp.concatenate(lines, axis=1)
 
     def contract(placed, basis):
@@ -292,22 +299,22 @@
     def unfold(total):
         return total[0:32, 0:128] + (total[0:32, 128:256] + total[32:64, 0:128]) + total[32:64, 128:256]
 
-    def backward(par, react):
-        def one(r, carry):
+    def backward(par, react, arriving=True):
+        def four(high, carry, first):
             total_a, total_d = carry
-            z_a, z_d = react(r)
-            total_a += contract(collect(par, r, z_a, got_a), basis_a[r])
-            total_d += contract(collect(par, r, z_d, got_d), basis_d[r])
+            for low in range(4):
+                r = 4 * high + low
+                if arriving and not (first and low == 0):
+                    wait_swapped(par, r)
+                z_a, z_d = react(r)
+                total_a += contract(collect(par, r, z_a, got_a), basis_a[r])
+                total_d += contract(collect(par, r, z_d, got_d), basis_d[r])
             return total_a, total_d
 
-        def step(r, carry):
-            pltpu.make_async_copy(theirs_a.at[par, r], theirs_a.at[par, r], swap_sem.at[par, 0, r]).wait()
-            pltpu.make_async_copy(theirs_d.at[par, r], theirs_d.at[par, r], swap_sem.at[par, 1, r]).wait()
-            return one(r, carry)
-
         zero = jnp.zeros((64, 256), F32)
-        total_a, total_d = lax.fori_loop(1, 16, step, one(0, (zero, zero)))
-        wait_sent(par)
+        total_a, total_d = lax.fori_loop(1, 4, lambda k, c: four(k, c, False), four(0, (zero, zero), True))
+        if arriving:
+            wait_sent(par)
         return jnp.concatenate([unfold(total_a), unfold(total_d)], axis=0)
 
     def wait_sent(par):
@@ -342,12 +349,7 @@
         return react
 
     def take(par, n):
-        def step(r, carry):
-            pltpu.make_async_copy(theirs_a.at[par, r], theirs_a.at[par, r], swap_sem.at[par, 0, r]).wait()
-            pltpu.make_async_copy(theirs_d.at[par, r], theirs_d.at[par, r], swap_sem.at[par, 1, r]).wait()
-            return carry
-
-        lax.fori_loop(1, 16, step, 0)
+        lax.fori_loop(1, 16, lambda r, c: (wait_swapped(par, r), c)[1], 0)
         wait_sent(par)
         y_a[n] = mine_a[par] - theirs_a[par]
         y_d[n] = theirs_d[par] - mine_d[par]
@@ -359,7 +361,7 @@
         def send(k, carry):
             pltpu.make_async_remote_copy(
                 src_ref=part.at[n], dst_ref=ring_z.at[n, k], send_sem=sum_send.at[n, 0], recv_sem=sum_sem.at[n, 0],
-                device_id=(p, (q + 8 - k) % 8), device_id_type=MESH,
+                device_id=(p, rem(q + 8 - k, 8)), device_id_type=MESH,
             ).start()
             return carry
 
@@ -369,15 +371,15 @@
     def sum_second(n):
         whole = ring_z.at[n, pl.ds(1, 7)]
         pltpu.make_async_copy(whole, whole, sum_sem.at[n, 0]).wait()
-        total = ring_z[n, (8 - q) % 8]
+        total = ring_z[n, rem(8 - q, 8)]
         for k in range(1, 8):
-            total = total + ring_z[n, (k + 8 - q) % 8]
+            total = total + ring_z[n, rem(k + 8 - q, 8)]
         part_z[n] = total
 
         def send(k, carry):
             pltpu.make_async_remote_copy(
                 src_ref=part_z.at[n], dst_ref=ring_xy.at[n, k], send_sem=sum_send.at[n, 1], recv_sem=sum_sem.at[n, 1],
-                device_id=((p + 16 - k) % 16, q), device_id_type=MESH,
+                device_id=(rem(p + 16 - k, 16), q), device_id_type=MESH,
             ).start()
             return carry
 
@@ -387,9 +389,9 @@
     def sum_last(n):
         whole = ring_xy.at[n, pl.ds(1, 15)]
         pltpu.make_async_copy(whole, whole, sum_sem.at[n, 1]).wait()
-        total = ring_xy[n, (16 - p) % 16]
+        total = ring_xy[n, rem(16 - p, 16)]
         for k in range(1, 16):
-            total = total + ring_xy[n, (k + 16 - p) % 16]
+            total = total + ring_xy[n, rem(k + 16 - p, 16)]
         pltpu.make_async_copy(ring_z.at[n, pl.ds(1, 7)], ring_z.at[n, pl.ds(1, 7)], sum_send.at[n, 0]).wait()
         pltpu.make_async_copy(whole, whole, sum_send.at[n, 1]).wait()
         total = jnp.sum(total, axis=1, keepdims=True)
@@ -414,18 +416,7 @@
             gradient = backward(par, misfit(par, True))
             par = 1 - par
         else:
-            react = misfit(par, False)
-
-            def gather(r, carry):
-                z_a, z_d = react(r)
-                return (
-                    carry[0] + contract(collect(0, r, z_a, got_a), basis_a[r]),
-                    carry[1] + contract(collect(0, r, z_d, got_d), basis_d[r]),
-                )
-
-            zero = jnp.zeros((64, 256), F32)
-            total_a, total_d = lax.fori_loop(0, 16, gather, (zero, zero))
-            gradient = jnp.concatenate([unfold(total_a), unfold(total_d)], axis=0)
+            gradient = backward(par, misfit(par, False), arriving=False)
         r0 = gradient - DAMPING * state
         vecs[0] = state
         vecs[1] = r0

time: 106 us -> 91 us (0.86)
  Pallas kernels: 103 us -> 88.2 us
    pallas_call x1, Pallas kernels: 103 us -> 88.2 us  [body(): pl.pallas_call(kernel, out_shape=(jax.ShapeDtypeStruct((32, 128), F32),)...]
where the time goes in v2:
time: 91 us; the launch traced here: 90.8 us
  Pallas kernels  88.2 us (97%)
  local copies, waits for them, and re-layouts  1.94 us (2%)
    pallas_call x1, Pallas kernels, body(): pl.pallas_call(kernel, out_shape=(jax.ShapeDtypeStruct((32, 128), F32),)...  88.2 us
    unnamed x4, local copies, waits for them, and re-layouts  1.94 us

profile of v2, /device:TPU:0, one launch (start us, length us, event | category | flops | bytes accessed | tf_op | source)
XLA Modules:
  0.0 90.8 jit_solution(13076635813774131763)
XLA Ops:
  0.6 88.2 %adjust.1 = (f32[32,128]{1,0:T(8,128)}, f32[32,128]{1,0:T(8,128)}) custom-call(f32[32,128]{1,0:T(8,128)} %coef_a.1, f32[32,128]{1,0:T(8,128)} %coef_d.1, s32[64,128]{1,0:T(8,128)} %ids_a.1, s32[64,128]{1,0:T(8,128)} %ids_d.1, f32[64,128]{1,0:T(8,128)} %time_a.1, f32[64,128]{1,0:T(8,128)} %time_d.1, f32[64,128]{1,0:T(8,128)} %height.1, s32[1,64]{1,0:T(1,128)} %bitcast.1), custom_call_target="tpu_custom_call" | custom-call | tf_op jit(solution)/shard_map/adjust/pallas_call | solution.py:493
  88.8 0.0 copy-start
  88.9 1.3 %copy.12 = f32[32,128]{1,0:T(8,128)} copy(f32[32,128]{1,0:T(8,128)} %get-tuple-element.4) | data formatting | bytes 32768
  90.2 0.0 copy-done
  90.2 0.6 copy.13
Async XLA Ops:
  88.8 1.3 %copy-start = (f32[32,128]{1,0:T(8,128)S(1)}, f32[32,128]{1,0:T(8,128)}, u32[]{:S(2)}) copy-start(f32[32,128]{1,0:T(8,128)} %get-tuple-element.5) | copy-start | bytes 49156

commit v3 on v2

--- a/solution.py
+++ b/solution.py
@@ -65,12 +65,16 @@
 
 
 def slot_between(first, second):
-    d = [rem(a + b, 2) for a, b in zip(first, second)]
-    return 8 * d[0] + 4 * d[1] + 2 * d[2] + d[3]
-
-
-def partner(cube, member, high, low):
-    d = (div(high, 2), rem(high, 2), div(low, 2), rem(low, 2))
+    dy, dx, dz, dc = [rem(a + b, 2) for a, b in zip(first, second)]
+    mid = rem(dy + dx, 2)
+    group = mid * (1 + dz) + (1 - mid) * 3 * dy
+    return 4 * group + 2 * (mid * dy + (1 - mid) * dz) + dc
+
+
+def partner(cube, member, group, low):
+    upper, core = low // 2, low % 2
+    mid, top = rem(div(group + 1, 2), 2), div(group, 3)
+    d = (mid * upper + top, mid * (1 - upper) + top, mid * (group - 1) + (1 - mid) * upper, core)
     return device_of(cube, tuple(m if isinstance(b, int) and b == 0 else rem(m + b, 2) for m, b in zip(member, d)))
 
 
@@ -107,9 +111,9 @@
 
 def kernel(
     coef_a, coef_d, ids_a, ids_d, time_a, time_d, height, fill,
-    out_a, out_d,
+    out,
     turned, stage_a, stage_d, got_a, got_d, coefs,
-    basis_a, basis_d, mine_a, mine_d, theirs_a, theirs_d,
+    basis_a, basis_d, mine, theirs,
     weight_a, weight_d, err_a, err_d, y_a, y_d, vecs,
     part, ring_z, part_z, ring_xy, home_a, home_d,
     init_sem_a, init_sem_d, init_send, coef_sem, coef_send,
@@ -166,6 +170,17 @@
         for k in range(2):
             stage_d[i, k] = turned[3 + k, pl.ds(i, 4, stride=16), :]
 
+    sends = []
+    for k in range(8):
+        for kind, shift in ((0, q), (1, p)):
+            j = rem(k + shift, 8)
+            a_home = asc_home(j, p)
+            for h in range(2):
+                d_home = desc_home(j, h, q)
+                r = slot_between(a_home[1], d_home[1])
+                sends.append((kind, j + 8 * h, r, at(d_home) if kind else at(a_home)))
+    home_of_a, home_of_d = at(asc_home(q, p)), at(desc_home(rem(p, 8), div(p, 8), q))
+
     pl.semaphore_wait(barrier, 8 + 16 + 15 + 7 + 15 + 2)
 
     def coef_copy(side, source, device):
@@ -174,33 +189,16 @@
             device_id=device, device_id_type=MESH,
         )
 
-    send_coef_a = coef_copy(0, coef_a, at(asc_home(q, p)))
-    send_coef_d = coef_copy(1, coef_d, at(desc_home(rem(p, 8), div(p, 8), q)))
+    for kind, i, r, device in sends:
+        stage, got, arrived = ((stage_a, got_a, init_sem_a), (stage_d, got_d, init_sem_d))[kind]
+        pltpu.make_async_remote_copy(
+            src_ref=stage.at[i], dst_ref=got.at[r], send_sem=init_send.at[kind], recv_sem=arrived.at[r],
+            device_id=device, device_id_type=MESH,
+        ).start()
+    send_coef_a = coef_copy(0, coef_a, home_of_a)
+    send_coef_d = coef_copy(1, coef_d, home_of_d)
     send_coef_a.start()
     send_coef_d.start()
-
-    def send_slots(k, carry):
-        j = rem(k + q, 8)
-        a_home = asc_home(j, p)
-        for h in range(2):
-            d_home = desc_home(j, h, q)
-            r = slot_between(a_home[1], d_home[1])
-            pltpu.make_async_remote_copy(
-                src_ref=stage_a.at[j + 8 * h], dst_ref=got_a.at[r], send_sem=init_send.at[0], recv_sem=init_sem_a.at[r],
-                device_id=at(a_home), device_id_type=MESH,
-            ).start()
-        j = rem(k + p, 8)
-        a_home = asc_home(j, p)
-        for h in range(2):
-            d_home = desc_home(j, h, q)
-            r = slot_between(a_home[1], d_home[1])
-            pltpu.make_async_remote_copy(
-                src_ref=stage_d.at[j + 8 * h], dst_ref=got_d.at[r], send_sem=init_send.at[1], recv_sem=init_sem_d.at[r],
-                device_id=at(d_home), device_id_type=MESH,
-            ).start()
-        return carry
-
-    lax.fori_loop(0, 8, send_slots, 0)
 
     frequency = (lax.broadcasted_iota(jnp.int32, (8, 128), 0) + 1).astype(F32)
     arc = lax.broadcasted_iota(jnp.int32, (32, 128), 0).astype(F32)
@@ -226,7 +224,7 @@
             [jnp.concatenate([high, high], axis=1), jnp.concatenate([low, low], axis=1)], axis=0
         )
 
-    def apply(r, left, got, basis, mine, par, take_height):
+    def apply(r, left, got, basis, kind, par, take_height):
         terms = jnp.dot(left, basis[r], preferred_element_type=F32)
         terms = terms[0:32] + terms[32:64]
         for l in range(4):
@@ -234,54 +232,49 @@
             line = fold(jnp.where(ids == arc, terms[:, 128 * l : 128 * (l + 1)], 0.0))
             if take_height:
                 line = line - got[r, 2, l : l + 1, :]
-            mine[par, r, l : l + 1, :] = line
+            mine[par, r, kind, l : l + 1, :] = line
 
     def swap(par, high, low):
         device = partner(cube, member, high, low)
         r = 4 * high + low
-        for mine, theirs, mine_kind in ((mine_a, theirs_d, 0), (mine_d, theirs_a, 1)):
-            pltpu.make_async_remote_copy(
-                src_ref=mine.at[par, r], dst_ref=theirs.at[par, r],
-                send_sem=swap_send.at[par, mine_kind], recv_sem=swap_sem.at[par, 1 - mine_kind, r],
-                device_id=device, device_id_type=MESH,
-            ).start()
+        pltpu.make_async_remote_copy(
+            src_ref=mine.at[par, r], dst_ref=theirs.at[par, r], send_sem=swap_send.at[par], recv_sem=swap_sem.at[par, r],
+            device_id=device, device_id_type=MESH,
+        ).start()
 
     def wait_swapped(par, r):
-        for k, theirs in enumerate((theirs_a, theirs_d)):
-            pltpu.make_async_copy(theirs.at[par, r], theirs.at[par, r], swap_sem.at[par, k, r]).wait()
-
-    def forward(par, vector, build):
+        pltpu.make_async_copy(theirs.at[par, r], theirs.at[par, r], swap_sem.at[par, r]).wait()
+
+    def forward(par, vector, build=False, gathered=True):
         left_a, left_d = left_of(vector[0:32]), left_of(vector[32:64])
 
-        def prepare(r):
+        def arrive(r):
             pltpu.make_async_copy(got_a.at[r], got_a.at[r], init_sem_a.at[r]).wait()
             pltpu.make_async_copy(got_d.at[r], got_d.at[r], init_sem_d.at[r]).wait()
-            make_basis(r, got_a, basis_a)
-            make_basis(r, got_d, basis_d)
 
         def four(high):
+            for low in range(4 if build else 0):
+                arrive(4 * high + low)
             for low in range(3, -1, -1):
                 r = 4 * high + low
-                apply(r, left_a, got_a, basis_a, mine_a, par, build)
-                apply(r, left_d, got_d, basis_d, mine_d, par, False)
+                if build:
+                    make_basis(r, got_a, basis_a)
+                    make_basis(r, got_d, basis_d)
+                apply(r, left_a, got_a, basis_a, 0, par, build)
+                apply(r, left_d, got_d, basis_d, 1, par, False)
 
         def step(k, carry):
-            high = 3 - k
-            if build:
-                lax.fori_loop(4 * high, 4 * high + 4, lambda r, c: (prepare(r), c)[1], 0)
+            high = 3 - rem(2 * k, 3) if gathered else 3 - k
             four(high)
             for low in range(3, -1, -1):
                 swap(par, high, low)
             return carry
 
         lax.fori_loop(0, 3, step, 0)
-        if build:
-            lax.fori_loop(0, 4, lambda r, c: (prepare(r), c)[1], 0)
         four(0)
         for low in range(3, 0, -1):
             swap(par, 0, low)
-        theirs_a[par, 0] = mine_d[par, 0]
-        theirs_d[par, 0] = mine_a[par, 0]
+        theirs[par, 0] = mine[par, 0]
 
     def collect(par, r, z, got):
         high = z.astype(BF16).astype(F32)
@@ -299,34 +292,44 @@
     def unfold(total):
         return total[0:32, 0:128] + (total[0:32, 128:256] + total[32:64, 0:128]) + total[32:64, 128:256]
 
-    def backward(par, react, arriving=True):
-        def four(high, carry, first):
+    def backward(par, react, arriving=True, between=None):
+        def some(high, lows, carry):
             total_a, total_d = carry
-            for low in range(4):
+            if arriving:
+                for low in lows:
+                    wait_swapped(par, 4 * high + low)
+            for low in lows:
                 r = 4 * high + low
-                if arriving and not (first and low == 0):
-                    wait_swapped(par, r)
                 z_a, z_d = react(r)
                 total_a += contract(collect(par, r, z_a, got_a), basis_a[r])
                 total_d += contract(collect(par, r, z_d, got_d), basis_d[r])
             return total_a, total_d
 
         zero = jnp.zeros((64, 256), F32)
-        total_a, total_d = lax.fori_loop(1, 4, lambda k, c: four(k, c, False), four(0, (zero, zero), True))
+        z_a, z_d = react(0)
+        carry = contract(collect(par, 0, z_a, got_a), basis_a[0]), contract(collect(par, 0, z_d, got_d), basis_d[0])
+        carry = some(1, range(4), carry)
+        if between:
+            between()
+        carry = some(0, range(1, 4), carry)
+        for high in (2, 3):
+            carry = some(high, range(4), carry)
+        total_a, total_d = carry
         if arriving:
             wait_sent(par)
         return jnp.concatenate([unfold(total_a), unfold(total_d)], axis=0)
 
     def wait_sent(par):
-        for k, mine in enumerate((mine_a, mine_d)):
-            sent = mine.at[par, pl.ds(1, 15)]
-            pltpu.make_async_copy(sent, sent, swap_send.at[par, k]).wait()
+        sent = mine.at[par, pl.ds(1, 15)]
+        pltpu.make_async_copy(sent, sent, swap_send.at[par]).wait()
+
+    def pairs(par, r):
+        return mine[par, r, 0] - theirs[par, r, 1], theirs[par, r, 0] - mine[par, r, 1]
 
     def misfit(par, first):
         def react(r):
             if first:
-                err_a[r] = mine_a[par, r] - theirs_a[par, r]
-                err_d[r] = theirs_d[par, r] - mine_d[par, r]
+                err_a[r], err_d[r] = pairs(par, r)
             zs = []
             for err, got, weight in ((err_a, got_a, weight_a), (err_d, got_d, weight_d)):
                 lives = jnp.where(got[r, 0] >= 0.0, 1.0, 0.0)
@@ -340,8 +343,7 @@
 
     def image(par, n):
         def react(r):
-            a = mine_a[par, r] - theirs_a[par, r]
-            d = theirs_d[par, r] - mine_d[par, r]
+            a, d = pairs(par, r)
             y_a[n, r] = a
             y_d[n, r] = d
             return weight_a[r] * a, -(weight_d[r] * d)
@@ -351,51 +353,49 @@
     def take(par, n):
         lax.fori_loop(1, 16, lambda r, c: (wait_swapped(par, r), c)[1], 0)
         wait_sent(par)
-        y_a[n] = mine_a[par] - theirs_a[par]
-        y_d[n] = theirs_d[par] - mine_d[par]
+        y_a[n] = mine[par, :, 0] - theirs[par, :, 1]
+        y_d[n] = theirs[par, :, 0] - mine[par, :, 1]
 
     def sum_first(n, rows):
         rows = rows + [jnp.zeros((1, 128), F32)] * (8 - len(rows))
-        part[n] = jnp.concatenate(rows, axis=0)
-
-        def send(k, carry):
+        sums = jnp.sum(jnp.concatenate(rows, axis=0), axis=1, keepdims=True)
+        own = lax.broadcasted_iota(jnp.int32, (8, 128), 0) == lax.broadcasted_iota(jnp.int32, (8, 128), 1)
+        line = fold(jnp.where(own, jnp.broadcast_to(sums, (8, 128)), 0.0))
+        part[n] = line
+        for k in (4, 3, 5, 2, 6, 1, 7):
             pltpu.make_async_remote_copy(
-                src_ref=part.at[n], dst_ref=ring_z.at[n, k], send_sem=sum_send.at[n, 0], recv_sem=sum_sem.at[n, 0],
-                device_id=(p, rem(q + 8 - k, 8)), device_id_type=MESH,
+                src_ref=part.at[n], dst_ref=ring_z.at[n, q], send_sem=sum_send.at[n, 0], recv_sem=sum_sem.at[n, 0],
+                device_id=(p, rem(q + k, 8)), device_id_type=MESH,
             ).start()
-            return carry
-
-        lax.fori_loop(1, 8, send, 0)
-        ring_z[n, 0] = part[n]
+        ring_z[n, q] = line
+
+    def added(ring, n, count):
+        lines = [ring[n, k] for k in range(count)]
+        while len(lines) > 1:
+            lines = [a + b for a, b in zip(lines[0::2], lines[1::2])]
+        return lines[0]
 
     def sum_second(n):
-        whole = ring_z.at[n, pl.ds(1, 7)]
+        whole = ring_z.at[n, pl.ds(0, 7)]
         pltpu.make_async_copy(whole, whole, sum_sem.at[n, 0]).wait()
-        total = ring_z[n, rem(8 - q, 8)]
-        for k in range(1, 8):
-            total = total + ring_z[n, rem(k + 8 - q, 8)]
+        total = added(ring_z, n, 8)
         part_z[n] = total
-
-        def send(k, carry):
+        for k in (10, 6, 2, 14, 8, 9, 7, 5, 11, 3, 13, 1, 15, 4, 12):
             pltpu.make_async_remote_copy(
-                src_ref=part_z.at[n], dst_ref=ring_xy.at[n, k], send_sem=sum_send.at[n, 1], recv_sem=sum_sem.at[n, 1],
-                device_id=(rem(p + 16 - k, 16), q), device_id_type=MESH,
+                src_ref=part_z.at[n], dst_ref=ring_xy.at[n, p], send_sem=sum_send.at[n, 1], recv_sem=sum_sem.at[n, 1],
+                device_id=(rem(p + k, 16), q), device_id_type=MESH,
             ).start()
-            return carry
-
-        lax.fori_loop(1, 16, send, 0)
-        ring_xy[n, 0] = total
+        ring_xy[n, p] = total
 
     def sum_last(n):
-        whole = ring_xy.at[n, pl.ds(1, 15)]
+        whole = ring_xy.at[n, pl.ds(0, 15)]
         pltpu.make_async_copy(whole, whole, sum_sem.at[n, 1]).wait()
-        total = ring_xy[n, rem(16 - p, 16)]
-        for k in range(1, 16):
-            total = total + ring_xy[n, rem(k + 16 - p, 16)]
-        pltpu.make_async_copy(ring_z.at[n, pl.ds(1, 7)], ring_z.at[n, pl.ds(1, 7)], sum_send.at[n, 0]).wait()
-        pltpu.make_async_copy(whole, whole, sum_send.at[n, 1]).wait()
-        total = jnp.sum(total, axis=1, keepdims=True)
-        return [total[k : k + 1, 0:1] for k in range(8)]
+        total = added(ring_xy, n, 16)
+        return [jnp.broadcast_to(total[:, k : k + 1], (1, 128)) for k in range(8)]
+
+    def sum_sent(n):
+        for stage, whole in ((0, ring_z.at[n, pl.ds(0, 7)]), (1, ring_xy.at[n, pl.ds(0, 15)])):
+            pltpu.make_async_copy(whole, whole, sum_send.at[n, stage]).wait()
 
     def send_home(k):
         for side, buffer, device in ((0, home_a, (my_asc, me_class)), (1, home_d, (my_i, my_q))):
@@ -412,44 +412,40 @@
     forward(par, state, True)
     for step in range(2):
         last = step == 1
-        if step == 0:
-            gradient = backward(par, misfit(par, True))
-            par = 1 - par
-        else:
-            gradient = backward(par, misfit(par, False), arriving=False)
-        r0 = gradient - DAMPING * state
         vecs[0] = state
-        vecs[1] = r0
-        forward(par, r0, False)
         if last:
             send_home(0)
-            send_home(1)
+        gradient = backward(par, misfit(par, not last), arriving=not last)
+        if not last:
+            par = 1 - par
+        r0 = gradient - DAMPING * state
+        vecs[1] = r0
+        forward(par, r0)
         v1 = backward(par, image(par, 0)) + DAMPING * r0
         par = 1 - par
         vecs[2] = v1
         sum_first(2 * step, [fold(r0 * r0), fold(r0 * v1)])
-        forward(par, v1, False)
+        if last:
+            send_home(1)
+        forward(par, v1)
+        v2 = backward(par, image(par, 1), between=functools.partial(sum_second, 2 * step)) + DAMPING * v1
+        par = 1 - par
+        vecs[3] = v2
         if last:
             send_home(2)
-        sum_second(2 * step)
-        v2 = backward(par, image(par, 1)) + DAMPING * v1
-        par = 1 - par
-        vecs[3] = v2
-        forward(par, v2, False)
-        if last:
-            send_home(3)
+        forward(par, v2, gathered=False)
         rr0, mu0 = sum_last(2 * step)[0:2]
         a0 = rr0 / mu0
         r1 = r0 - a0 * v1
         u1 = v1 - a0 * v2
+        lines = [fold(r1 * r1), fold(r1 * u1), fold(r1 * v1), fold(u1 * u1), fold(u1 * v1), fold(v1 * v1)]
         take(par, 2)
         par = 1 - par
         ju = y_a[1] - a0 * y_a[2]
         curve = jnp.sum(weight_a[...] * ju * ju, axis=0)
-        sum_first(
-            2 * step + 1,
-            [fold(r1 * r1), fold(r1 * u1), fold(r1 * v1), fold(u1 * u1), fold(u1 * v1), fold(v1 * v1), fold(curve)],
-        )
+        sum_first(2 * step + 1, lines + [fold(curve)])
+        if last:
+            send_home(3)
         sum_second(2 * step + 1)
         rr1, ru, rv, uu, uv, vv, wuu = sum_last(2 * step + 1)[0:7]
         b1 = rr1 / rr0
@@ -477,24 +473,26 @@
 
     send_coef_a.wait_send()
     send_coef_d.wait_send()
+    for n in range(4):
+        sum_sent(n)
     pltpu.make_async_copy(stage_a, stage_a, init_send.at[0]).wait()
     pltpu.make_async_copy(stage_d, stage_d, init_send.at[1]).wait()
-    for side, (buffer, out) in enumerate(((home_a, out_a), (home_d, out_d))):
+    for side, buffer in enumerate((home_a, home_d)):
         for k in range(4):
             pltpu.make_async_copy(buffer.at[k], buffer.at[k], home_sem.at[side, k]).wait()
             pltpu.make_async_copy(buffer.at[k], buffer.at[k], home_send.at[side, k]).wait()
-        out[...] = buffer[0] + (k0 * buffer[1] + k1 * buffer[2] + k2 * buffer[3])
+        out[32 * side : 32 * side + 32] = buffer[0] + (k0 * buffer[1] + k1 * buffer[2] + k2 * buffer[3])
 
 
 def body(coef_a, coef_d, cross_a, cross_d, time_a, time_d, height, fill):
     vmem = pl.BlockSpec(memory_space=pltpu.VMEM)
     values = pltpu.VMEM((SLOTS, 4, 128), F32)
     dma = pltpu.SemaphoreType.DMA
-    return pl.pallas_call(
+    out = pl.pallas_call(
         kernel,
-        out_shape=(jax.ShapeDtypeStruct((32, 128), F32),) * 2,
+        out_shape=jax.ShapeDtypeStruct((64, 128), F32),
         in_specs=[vmem] * 8,
-        out_specs=(vmem, vmem),
+        out_specs=vmem,
         scratch_shapes=[
             pltpu.VMEM((5, 64, 128), F32),
             pltpu.VMEM((16, 3, 4, 128), F32),
@@ -504,10 +502,8 @@
             pltpu.VMEM((2, 32, 128), F32),
             pltpu.VMEM((SLOTS, 256, 512), BF16),
             pltpu.VMEM((SLOTS, 256, 512), BF16),
-            pltpu.VMEM((2, SLOTS, 4, 128), F32),
-            pltpu.VMEM((2, SLOTS, 4, 128), F32),
-            pltpu.VMEM((2, SLOTS, 4, 128), F32),
-            pltpu.VMEM((2, SLOTS, 4, 128), F32),
+            pltpu.VMEM((2, SLOTS, 2, 4, 128), F32),
+            pltpu.VMEM((2, SLOTS, 2, 4, 128), F32),
             values,
             values,
             values,
@@ -515,10 +511,10 @@
             pltpu.VMEM((3, SLOTS, 4, 128), F32),
             pltpu.VMEM((3, SLOTS, 4, 128), F32),
             pltpu.VMEM((4, 64, 128), F32),
-            pltpu.VMEM((4, 8, 128), F32),
-            pltpu.VMEM((4, 8, 8, 128), F32),
-            pltpu.VMEM((4, 8, 128), F32),
-            pltpu.VMEM((4, 16, 8, 128), F32),
+            pltpu.VMEM((4, 1, 128), F32),
+            pltpu.VMEM((4, 8, 1, 128), F32),
+            pltpu.VMEM((4, 1, 128), F32),
+            pltpu.VMEM((4, 16, 1, 128), F32),
             pltpu.VMEM((4, 32, 128), F32),
             pltpu.VMEM((4, 32, 128), F32),
             dma((SLOTS,)),
@@ -526,8 +522,8 @@
             dma((2,)),
             dma((2,)),
             dma((2,)),
-            dma((2, 2, SLOTS)),
-            dma((2, 2)),
+            dma((2, SLOTS)),
+            dma((2,)),
             dma((4, 2)),
             dma((4, 2)),
             dma((2, 4)),
@@ -536,6 +532,7 @@
         compiler_params=pltpu.CompilerParams(collective_id=0, has_side_effects=True),
         name="adjust",
     )(coef_a, coef_d, cross_a, cross_d, time_a, time_d, height, fill.reshape(1, -1))
+    return out[0:32], out[32:64]
 
 
 def solution(mesh):

time: 91 us -> 84.4 us (0.927)
  Pallas kernels: 88.2 us -> 82.1 us
    pallas_call x1, Pallas kernels: 88.2 us -> 82.1 us  [body(): pl.pallas_call(kernel, out_shape=jax.ShapeDtypeStruct((64, 128), F32), in...]
    unnamed x4 -> x0, local copies, waits for them, and re-layouts: 1.94 us -> none
    slice x0 -> x1, local copies, waits for them, and re-layouts: none -> 1.35 us  [body(): return (out[0:32], out[32:64])]
where the time goes in v3:
time: 84.4 us; the launch traced here: 84.1 us
  Pallas kernels  82.1 us (97%)
  local copies, waits for them, and re-layouts  1.35 us (2%)
    pallas_call x1, Pallas kernels, body(): pl.pallas_call(kernel, out_shape=jax.ShapeDtypeStruct((64, 128), F32), in...  82.1 us

profile of v3, /device:TPU:0, one launch (start us, length us, event | category | flops | bytes accessed | tf_op | source)
XLA Modules:
  0.0 84.1 jit_solution(10842056172942809782)
XLA Ops:
  0.6 82.1 %adjust.1 = f32[64,128]{1,0:T(8,128)} custom-call(f32[32,128]{1,0:T(8,128)} %coef_a.1, f32[32,128]{1,0:T(8,128)} %coef_d.1, s32[64,128]{1,0:T(8,128)} %ids_a.1, s32[64,128]{1,0:T(8,128)} %ids_d.1, f32[64,128]{1,0:T(8,128)} %time_a.1, f32[64,128]{1,0:T(8,128)} %time_d.1, f32[64,128]{1,0:T(8,128)} %height.1, s32[1,64]{1,0:T(1,128)} %bitcast.1), custom_call_target="tpu_custom_call" | custom-call | tf_op jit(solution)/shard_map/adjust/pallas_call | solution.py:491
  82.8 1.3 %fusion = (f32[32,128]{1,0:T(8,128)}, f32[32,128]{1,0:T(8,128)}) fusion(f32[64,128]{1,0:T(8,128)} %adjust.1), kind=kLoop, calls=%fused_computation | loop fusion | bytes 65536 | tf_op jit(solution)/shard_map/slice | solution.py:535

commit v4 on v3

--- a/solution.py
+++ b/solution.py
@@ -263,17 +263,10 @@
                 apply(r, left_a, got_a, basis_a, 0, par, build)
                 apply(r, left_d, got_d, basis_d, 1, par, False)
 
-        def step(k, carry):
-            high = 3 - rem(2 * k, 3) if gathered else 3 - k
+        for high in (3, 1, 0, 2):
             four(high)
-            for low in range(3, -1, -1):
+            for low in range(3, -1 if high else 0, -1):
                 swap(par, high, low)
-            return carry
-
-        lax.fori_loop(0, 3, step, 0)
-        four(0)
-        for low in range(3, 0, -1):
-            swap(par, 0, low)
         theirs[par, 0] = mine[par, 0]
 
     def collect(par, r, z, got):
@@ -312,7 +305,7 @@
         if between:
             between()
         carry = some(0, range(1, 4), carry)
-        for high in (2, 3):
+        for high in (3, 2):
             carry = some(high, range(4), carry)
         total_a, total_d = carry
         if arriving:

time: 84.4 us -> 84 us (level)
  no operation moved by 1% of the time
where the time goes in v4:
time: 84 us; the launch traced here: 83.8 us
  Pallas kernels  81.8 us (97%)
  local copies, waits for them, and re-layouts  1.35 us (2%)
    pallas_call x1, Pallas kernels, body(): pl.pallas_call(kernel, out_shape=jax.ShapeDtypeStruct((64, 128), F32), in...  81.8 us

profile of v4, /device:TPU:0, one launch (start us, length us, event | category | flops | bytes accessed | tf_op | source)
XLA Modules:
  0.0 83.8 jit_solution(7938451580348183569)
XLA Ops:
  0.6 81.8 %adjust.1 = f32[64,128]{1,0:T(8,128)} custom-call(f32[32,128]{1,0:T(8,128)} %coef_a.1, f32[32,128]{1,0:T(8,128)} %coef_d.1, s32[64,128]{1,0:T(8,128)} %ids_a.1, s32[64,128]{1,0:T(8,128)} %ids_d.1, f32[64,128]{1,0:T(8,128)} %time_a.1, f32[64,128]{1,0:T(8,128)} %time_d.1, f32[64,128]{1,0:T(8,128)} %height.1, s32[1,64]{1,0:T(1,128)} %bitcast.1), custom_call_target="tpu_custom_call" | custom-call | tf_op jit(solution)/shard_map/adjust/pallas_call | solution.py:484
  82.4 1.3 %fusion = (f32[32,128]{1,0:T(8,128)}, f32[32,128]{1,0:T(8,128)}) fusion(f32[64,128]{1,0:T(8,128)} %adjust.1), kind=kLoop, calls=%fused_computation | loop fusion | bytes 65536 | tf_op jit(solution)/shard_map/slice | solution.py:528

commit v5 on v4

--- a/solution.py
+++ b/solution.py
@@ -263,7 +263,7 @@
                 apply(r, left_a, got_a, basis_a, 0, par, build)
                 apply(r, left_d, got_d, basis_d, 1, par, False)
 
-        for high in (3, 1, 0, 2):
+        for high in (3, 1, 0, 2) if gathered else (3, 2, 1, 0):
             four(high)
             for low in range(3, -1 if high else 0, -1):
                 swap(par, high, low)

time: 84 us -> 83.5 us (level)
  no operation moved by 1% of the time
where the time goes in v5:
time: 83.5 us; the launch traced here: 83.2 us
  Pallas kernels  81.2 us (97%)
  local copies, waits for them, and re-layouts  1.35 us (2%)
    pallas_call x1, Pallas kernels, body(): pl.pallas_call(kernel, out_shape=jax.ShapeDtypeStruct((64, 128), F32), in...  81.2 us

profile of v5, /device:TPU:0, one launch (start us, length us, event | category | flops | bytes accessed | tf_op | source)
XLA Modules:
  0.0 83.2 jit_solution(10118678023787068667)
XLA Ops:
  0.6 81.2 %adjust.1 = f32[64,128]{1,0:T(8,128)} custom-call(f32[32,128]{1,0:T(8,128)} %coef_a.1, f32[32,128]{1,0:T(8,128)} %coef_d.1, s32[64,128]{1,0:T(8,128)} %ids_a.1, s32[64,128]{1,0:T(8,128)} %ids_d.1, f32[64,128]{1,0:T(8,128)} %time_a.1, f32[64,128]{1,0:T(8,128)} %time_d.1, f32[64,128]{1,0:T(8,128)} %height.1, s32[1,64]{1,0:T(1,128)} %bitcast.1), custom_call_target="tpu_custom_call" | custom-call | tf_op jit(solution)/shard_map/adjust/pallas_call | solution.py:484
  81.9 1.3 %fusion = (f32[32,128]{1,0:T(8,128)}, f32[32,128]{1,0:T(8,128)}) fusion(f32[64,128]{1,0:T(8,128)} %adjust.1), kind=kLoop, calls=%fused_computation | loop fusion | bytes 65536 | tf_op jit(solution)/shard_map/slice | solution.py:528
